TPU v7x, 256 devices: a whole 4x4x8 slice. The times are simulated.
256 devices in a mesh: col: 64 (over y, z, core), row: 4 (over x).
Axes of the slice: x: 4, y: 4, z: 8, core: 2. Of those that a mesh axis runs over, the one named last changes fastest.
Arguments:
- r_slab: float32 [1024, 16384], P('row', 'col'), may hold values from -4 to 8, as said below
- arc_rows: float32 [4096, 16384], P('row', 'col'), may hold values from -6 to 6
- arc_blocks: int32 [32, 64], P('row', 'col'), may hold values 0 or 1
Outputs:
- r_updated: float32 [1024, 16384], P('row', 'col')
Inputs may be any that keep to these rules, and one draw needn't show every extreme that they name: r_slab is zero wherever an entry's global column index is below its row index, and its diagonal is positive.
All inputs are finite; a program needn't handle non-finite values. No bound on the sum of `arc_blocks` on one device may be relied on, other than what follows from the above.
Results may differ from a plain program's by a relative error of at most 0.000098.
Values sent between devices are 32-bit elements; how exact they have to be, the bound alone decides.
A program may use at most 64 MiB of HBM per device.

v0:
```python
import jax
import jax.numpy as jnp
from jax import lax
from jax.sharding import PartitionSpec as P

B = 256
P_SIZE = 4
ARC_ROWS = 128


def spread(value, axis, source):
    kept = jnp.where(lax.axis_index(axis) == source, value, 0).astype(value.dtype)
    return lax.psum(kept, axis)


def inner_dot(left, right):
    return jnp.dot(left.T, right, precision=lax.Precision.HIGHEST)


def plain_dot(left, right):
    return jnp.dot(left, right, precision=lax.Precision.HIGHEST)


def upper_keep(row_start, height, columns, col_index, n_col):
    row_ids = row_start + lax.broadcasted_iota(jnp.int32, (height, columns), 0)
    col_ids = lax.broadcasted_iota(jnp.int32, (height, columns), 1)
    global_col = (col_ids // B * n_col + col_index) * B + col_ids % B
    return global_col >= row_ids


def on_device(r_slab, arc_rows, arc_blocks):
    n_col = lax.axis_size("col")
    col_index = lax.axis_index("col")
    row_index = lax.axis_index("row")
    n_arcs, blocks_here = arc_blocks.shape
    columns = arc_rows.shape[1]
    live = arc_blocks.astype(jnp.float32)
    masked = (arc_rows.reshape(n_arcs, ARC_ROWS, blocks_here, B) * live[:, None, :, None]).reshape(
        arc_rows.shape
    )
    stacked = jnp.concatenate([r_slab, masked], axis=0)
    result = jnp.zeros(r_slab.shape, jnp.float32)
    for panel_id in range(P_SIZE):
        owner = panel_id % n_col
        slot = panel_id // n_col
        local_panel = stacked
        gram = lax.psum(inner_dot(local_panel, local_panel), "row")
        lower = jnp.linalg.cholesky(gram)
        basis = jax.scipy.linalg.solve_triangular(lower, local_panel.T, lower=True).T
        basis = spread(basis, "col", owner)
        block_row = lax.psum(inner_dot(basis, stacked), "row")
        keep = upper_keep(panel_id * B, B, columns, col_index, n_col)
        block_row = jnp.where(keep, block_row, jnp.zeros_like(block_row))
        result = jnp.where(row_index == panel_id, block_row, result)
        if panel_id + 1 < P_SIZE:
            stacked = stacked - plain_dot(basis, block_row)
    return result


def solution(mesh):
    return jax.shard_map(
        on_device,
        mesh=mesh,
        in_specs=(P("row", "col"), P("row", "col"), P("row", "col")),
        out_specs=P("row", "col"),
        check_vma=False,
    )
```

profile of v0, /device:TPU:1, one launch (start us, length us, event | category | flops | bytes accessed | tf_op | source)
XLA Modules:
  0.0 1444.5 jit_solution(14369312113321616529)
XLA Ops:
  7.3 1.4 broadcast_multiply_fusion
  8.8 2.9 fusion.14
  12.4 47.9 %all-reduce.14.cloned.1.call-done = f32[256,256]{0,1:T(8,128)} async-done(((f32[256,256]{0,1:T(8,128)}), f32[256,256]{0,1:T(8,128)}) %all-reduce.14.cloned.1.call-update) | async-done | bytes 262160 | tf_op jit(solution)/shard_map/psum | solution.py:47
  62.4 11.7 cholesky.214
  74.1 9.8 custom-call.17
  84.5 11.7 cholesky.231
  98.4 4.3 while.8
  99.2 1.4 bitcast_dynamic-update-slice_fusion.8
  101.2 1.4 bitcast_dynamic-update-slice_fusion.8
  102.7 19.7 %custom-call.18 = f32[2,128,128]{1,2,0:T(8,128)S(1)} custom-call(f32[2,128,128]{2,1,0:T(8,128)S(1)} %get-tuple-element.33), custom_call_target="InvertDiagBlocksLowerTriangular" | custom-call | tf_op jit(solution)/shard_map/jit(_solve_triangular)/triangular_solve | solution.py:49
  123.1 1.2 convolution_subtract_fusion.6
  125.1 1.2 fusion
  126.4 188.2 %all-reduce.16.cloned.1.call-done = f32[1280,256]{0,1:T(8,128)} async-done(((f32[1280,256]{0,1:T(8,128)}), f32[1280,256]{0,1:T(8,128)}) %all-reduce.16.cloned.1.call-update) | async-done | bytes 1310736 | tf_op jit(solution)/shard_map/psum | solution.py:13
  314.6 3.3 fusion.12
  318.0 45.1 %all-reduce.18.cloned.1.call-done = f32[256,256]{1,0:T(8,128)} async-done(((f32[256,256]{1,0:T(8,128)}), f32[256,256]{1,0:T(8,128)}) %all-reduce.18.cloned.1.call-update) | async-done | bytes 262160 | tf_op jit(solution)/shard_map/psum | solution.py:51
  363.1 3.6 convolution_subtract_fusion.2
  366.7 2.9 fusion.109
  369.9 47.1 %all-reduce.20.cloned.1.call-done = f32[256,256]{0,1:T(8,128)} async-done(((f32[256,256]{0,1:T(8,128)}), f32[256,256]{0,1:T(8,128)}) %all-reduce.20.cloned.1.call-update) | async-done | bytes 262160 | tf_op jit(solution)/shard_map/psum | solution.py:47
  417.1 1.1 copy.7
  419.1 11.7 cholesky.248
  430.9 9.8 custom-call.19
  441.2 11.7 cholesky.265
  455.7 4.5 while.9
  456.7 1.4 bitcast_dynamic-update-slice_fusion.9
  458.8 1.4 bitcast_dynamic-update-slice_fusion.9
  460.2 19.7 %custom-call.20 = f32[2,128,128]{1,2,0:T(8,128)S(1)} custom-call(f32[2,128,128]{2,1,0:T(8,128)S(1)} %get-tuple-element.34), custom_call_target="InvertDiagBlocksLowerTriangular" | custom-call | tf_op jit(solution)/shard_map/jit(_solve_triangular)/triangular_solve | solution.py:49
  480.7 1.2 convolution_subtract_fusion.5
  482.7 1.2 fusion.1
  483.9 188.3 %all-reduce.22.cloned.1.call-done = f32[1280,256]{0,1:T(8,128)} async-done(((f32[1280,256]{0,1:T(8,128)}), f32[1280,256]{0,1:T(8,128)}) %all-reduce.22.cloned.1.call-update) | async-done | bytes 1310736 | tf_op jit(solution)/shard_map/psum | solution.py:13
  672.2 3.3 fusion.110
  675.5 45.2 %all-reduce.24.cloned.1.call-done = f32[256,256]{1,0:T(8,128)} async-done(((f32[256,256]{1,0:T(8,128)}), f32[256,256]{1,0:T(8,128)}) %all-reduce.24.cloned.1.call-update) | async-done | bytes 262160 | tf_op jit(solution)/shard_map/psum | solution.py:51
  720.7 3.6 convolution_subtract_fusion.1
  724.3 2.9 fusion.111
  727.5 47.2 %all-reduce.26.cloned.1.call-done = f32[256,256]{0,1:T(8,128)} async-done(((f32[256,256]{0,1:T(8,128)}), f32[256,256]{0,1:T(8,128)}) %all-reduce.26.cloned.1.call-update) | async-done | bytes 262160 | tf_op jit(solution)/shard_map/psum | solution.py:47
  774.7 1.1 copy.9
  776.8 11.7 cholesky.282
  788.6 9.8 custom-call.21
  798.9 11.7 cholesky.299
  813.4 4.3 while.10
  814.2 1.4 bitcast_dynamic-update-slice_fusion.10
  816.3 1.4 bitcast_dynamic-update-slice_fusion.10
  817.7 19.7 %custom-call.22 = f32[2,128,128]{1,2,0:T(8,128)S(1)} custom-call(f32[2,128,128]{2,1,0:T(8,128)S(1)} %get-tuple-element.35), custom_call_target="InvertDiagBlocksLowerTriangular" | custom-call | tf_op jit(solution)/shard_map/jit(_solve_triangular)/triangular_solve | solution.py:49
  838.2 1.2 convolution_subtract_fusion.4
  840.1 1.2 fusion.2
  841.4 188.3 %all-reduce.28.cloned.1.call-done = f32[1280,256]{0,1:T(8,128)} async-done(((f32[1280,256]{0,1:T(8,128)}), f32[1280,256]{0,1:T(8,128)}) %all-reduce.28.cloned.1.call-update) | async-done | bytes 1310736 | tf_op jit(solution)/shard_map/psum | solution.py:13
  1029.7 3.3 fusion.112
  1033.0 45.2 %all-reduce.30.cloned.1.call-done = f32[256,256]{1,0:T(8,128)} async-done(((f32[256,256]{1,0:T(8,128)}), f32[256,256]{1,0:T(8,128)}) %all-reduce.30.cloned.1.call-update) | async-done | bytes 262160 | tf_op jit(solution)/shard_map/psum | solution.py:51
  1078.2 3.6 convolution_subtract_fusion
  1081.8 2.9 fusion.113
  1085.3 47.0 %all-reduce.32.cloned.1.call-done = f32[256,256]{0,1:T(8,128)} async-done(((f32[256,256]{0,1:T(8,128)}), f32[256,256]{0,1:T(8,128)}) %all-reduce.32.cloned.1.call-update) | async-done | bytes 262160 | tf_op jit(solution)/shard_map/psum | solution.py:47
  1132.2 1.1 copy.11
  1134.3 11.7 cholesky.316
  1146.1 9.8 custom-call.23
  1156.4 11.7 cholesky.333
  1170.9 4.3 while.11
  1171.7 1.4 bitcast_dynamic-update-slice_fusion.11
  1173.7 1.4 bitcast_dynamic-update-slice_fusion.11
  1175.2 19.7 %custom-call.24 = f32[2,128,128]{1,2,0:T(8,128)S(1)} custom-call(f32[2,128,128]{2,1,0:T(8,128)S(1)} %get-tuple-element.36), custom_call_target="InvertDiagBlocksLowerTriangular" | custom-call | tf_op jit(solution)/shard_map/jit(_solve_triangular)/triangular_solve | solution.py:49
  1195.6 1.2 convolution_subtract_fusion.3
  1197.6 1.2 fusion.3
  1198.9 188.2 %all-reduce.34.cloned.1.call-done = f32[1280,256]{0,1:T(8,128)} async-done(((f32[1280,256]{0,1:T(8,128)}), f32[1280,256]{0,1:T(8,128)}) %all-reduce.34.cloned.1.call-update) | async-done | bytes 1310736 | tf_op jit(solution)/shard_map/psum | solution.py:13
  1387.1 3.3 fusion.114
  1390.4 45.2 %all-reduce.36.cloned.1.call-done = f32[256,256]{1,0:T(8,128)} async-done(((f32[256,256]{1,0:T(8,128)}), f32[256,256]{1,0:T(8,128)}) %all-reduce.36.cloned.1.call-update) | async-done | bytes 262160 | tf_op jit(solution)/shard_map/psum | solution.py:51
  1435.6 1.8 select_select_fusion.4
  (111 shorter events, 26.0 us)
Async XLA Ops:
  6.5 2.2 copy-start
  6.5 53.8 %all-reduce.14.cloned.1.call-start = ((), (), s32[]{:S(2)}) async-start(), calls=%async_computation | async-start | bytes 524288 | tf_op jit(solution)/shard_map/psum | solution.py:47
  11.7 302.9 %all-reduce.16.cloned.1.call-start = ((), (), s32[]{:S(2)}) async-start(), calls=%async_computation.1 | async-start | bytes 2621440 | tf_op jit(solution)/shard_map/psum | solution.py:13
  126.3 236.8 %all-reduce.18.cloned.1.call-start = ((), (), s32[]{:S(2)}) async-start(), calls=%async_computation.2 | async-start | bytes 524288 | tf_op jit(solution)/shard_map/psum | solution.py:51
  317.9 99.2 %all-reduce.20.cloned.1.call-start = ((), (), s32[]{:S(2)}) async-start(), calls=%async_computation.3 | async-start | bytes 524288 | tf_op jit(solution)/shard_map/psum | solution.py:47
  369.6 302.5 %all-reduce.22.cloned.1.call-start = ((), (), s32[]{:S(2)}) async-start(), calls=%async_computation.4 | async-start | bytes 2621440 | tf_op jit(solution)/shard_map/psum | solution.py:13
  483.9 236.9 %all-reduce.24.cloned.1.call-start = ((), (), s32[]{:S(2)}) async-start(), calls=%async_computation.5 | async-start | bytes 524288 | tf_op jit(solution)/shard_map/psum | solution.py:51
  675.5 99.3 %all-reduce.26.cloned.1.call-start = ((), (), s32[]{:S(2)}) async-start(), calls=%async_computation.6 | async-start | bytes 524288 | tf_op jit(solution)/shard_map/psum | solution.py:47
  727.3 302.4 %all-reduce.28.cloned.1.call-start = ((), (), s32[]{:S(2)}) async-start(), calls=%async_computation.7 | async-start | bytes 2621440 | tf_op jit(solution)/shard_map/psum | solution.py:13
  841.3 236.9 %all-reduce.30.cloned.1.call-start = ((), (), s32[]{:S(2)}) async-start(), calls=%async_computation.8 | async-start | bytes 524288 | tf_op jit(solution)/shard_map/psum | solution.py:51
  1032.9 99.3 %all-reduce.32.cloned.1.call-start = ((), (), s32[]{:S(2)}) async-start(), calls=%async_computation.9 | async-start | bytes 524288 | tf_op jit(solution)/shard_map/psum | solution.py:47
  1084.8 302.3 %all-reduce.34.cloned.1.call-start = ((), (), s32[]{:S(2)}) async-start(), calls=%async_computation.10 | async-start | bytes 2621440 | tf_op jit(solution)/shard_map/psum | solution.py:13
  1198.8 236.9 %copy-start.1 = (f32[256,256]{1,0:T(8,128)S(1)}, f32[256,256]{1,0:T(8,128)}, u32[]{:S(2)}) copy-start(f32[256,256]{1,0:T(8,128)} %all-reduce.18.cloned.1.call-done) | copy-start | bytes 786436
  1198.8 236.9 %copy-start.2 = (f32[256,256]{1,0:T(8,128)S(1)}, f32[256,256]{1,0:T(8,128)}, u32[]{:S(2)}) copy-start(f32[256,256]{1,0:T(8,128)} %all-reduce.24.cloned.1.call-done) | copy-start | bytes 786436
  1198.8 236.9 %copy-start.3 = (f32[256,256]{1,0:T(8,128)S(1)}, f32[256,256]{1,0:T(8,128)}, u32[]{:S(2)}) copy-start(f32[256,256]{1,0:T(8,128)} %all-reduce.30.cloned.1.call-done) | copy-start | bytes 786436
  1198.8 236.8 %all-reduce.36.cloned.1.call-start = ((), (), s32[]{:S(2)}) async-start(), calls=%async_computation.11 | async-start | bytes 524288 | tf_op jit(solution)/shard_map/psum | solution.py:51
Sparse Core Ops, SparseCore 0:
  11.8 48.4 all-reduce.13
  126.4 188.1 all-reduce.15
  318.0 45.0 all-reduce.17
  369.8 47.2 all-reduce.19
  484.0 188.1 all-reduce.21
  675.6 45.1 all-reduce.23
  727.4 47.2 all-reduce.25
  841.5 188.1 all-reduce.27
  1033.1 45.1 all-reduce.29
  1084.9 47.2 all-reduce.31
  1198.9 188.1 all-reduce.33
  1390.5 45.1 all-reduce.35
where the time goes:
time: 1450 us; the launch traced here: 1440 us
  waiting for transfers between devices  1120 us (77%)
  other arithmetic  230 us (16%)
  matrix products  48.3 us (3%)
  local copies, waits for them, and re-layouts  20.8 us (1%)
  between operations  19.7 us (1%)
    psum x4, waiting for transfers between devices, spread(): return lax.psum(kept, axis)  753 us
    psum x4, waiting for transfers between devices, on_device(): gram = lax.psum(inner_dot(local_panel, local_panel), 'row')  189 us
    psum x4, waiting for transfers between devices, on_device(): block_row = lax.psum(inner_dot(basis, stacked), 'row')  181 us
    another operation x27, other arithmetic, on_device(): lower = jnp.linalg.cholesky(gram)  138 us
    another operation x9, other arithmetic, on_device(): jax.scipy.linalg.solve_triangular(lower, local_panel.T, lower=True)  78.8 us
  transfers between devices with their start and end apart: 12, of which 12 were waited for; matrix products, arithmetic and copies ran while one was open for 0% of the time, Pallas kernels for 0%

commit v1 on v0

v1 whole, which is shorter than its diff:
```python
import jax
import jax.numpy as jnp
from jax import lax
from jax.sharding import PartitionSpec as P

B = 256
P_SIZE = 4
ARC_ROWS = 128
HI = lax.Precision.HIGHEST


def inner_dot(left, right):
    return lax.dot_general(left, right, (((0,), (0,)), ((), ())), precision=HI)


def plain_dot(left, right):
    return jnp.dot(left, right, precision=HI)


def on_device(r_slab, arc_rows, arc_blocks):
    n_col = lax.axis_size("col")
    col_index = lax.axis_index("col")
    row_index = lax.axis_index("row")
    n_arcs, blocks_here = arc_blocks.shape
    lead = P_SIZE * B
    live = arc_blocks.astype(jnp.float32)
    masked = (arc_rows.reshape(n_arcs, ARC_ROWS, blocks_here, B) * live[:, None, :, None]).reshape(
        arc_rows.shape
    )
    stacked = jnp.concatenate([r_slab, masked], axis=0)
    height = stacked.shape[0]
    part = height // n_col
    pieces = stacked.reshape(n_col, part, B)
    pieces = lax.all_to_all(pieces, "col", split_axis=0, concat_axis=0, tiled=True)
    mine = pieces[:P_SIZE]
    panels = lax.all_gather(mine, "col")
    panels = panels.transpose(0, 2, 1, 3).reshape(height, lead)
    share = lead // n_col
    own = lax.dynamic_slice(panels, (0, col_index * share), (height, share))
    gram_part = lax.psum(inner_dot(own, panels), "row")
    gram = lax.all_gather(gram_part, "col", tiled=True)
    rhs = lax.psum(inner_dot(panels, stacked), "row")
    lower = jnp.linalg.cholesky(gram, symmetrize_input=False)
    factor = jax.scipy.linalg.solve_triangular(lower, rhs, lower=True)
    mine_out = lax.dynamic_slice(factor, (row_index * B, 0), (B, B))
    row_ids = row_index * B + lax.broadcasted_iota(jnp.int32, (B, B), 0)
    col_ids = col_index * B + lax.broadcasted_iota(jnp.int32, (B, B), 1)
    return jnp.where(col_ids >= row_ids, mine_out, jnp.zeros_like(mine_out))


def solution(mesh):
    return jax.shard_map(
        on_device,
        mesh=mesh,
        in_specs=(P("row", "col"), P("row", "col"), P("row", "col")),
        out_specs=P("row", "col"),
        check_vma=False,
    )
```

time: 1450 us -> 647 us (0.45)
  waiting for transfers between devices: 1120 us -> 210 us
  blocking collectives: 0 us -> 52.7 us
  other arithmetic: 230 us -> 261 us
    psum x12 -> x1, waiting for transfers between devices: 1120 us -> 46.4 us  [on_device(): rhs = lax.psum(inner_dot(panels, stacked), 'row')]
    all_gather x0 -> x2, waiting for transfers between devices: none -> 163 us  [the longest x1 84.7 us: on_device(): gram = lax.all_gather(gram_part, 'col', tiled=True)]
    all_to_all x0 -> x1, blocking collectives: none -> 52.7 us  [on_device(): lax.all_to_all(pieces, 'col', split_axis=0, concat_axis=0, tiled=True)]
    another operation x36 -> x33, other arithmetic: 217 us -> 256 us  [the longest x30 173 us: on_device(): lower = jnp.linalg.cholesky(gram, symmetrize_input=False)]
    another operation x20 -> x29, matrix products: 12.8 us -> 35.4 us  [the longest x14 23.3 us: on_device(): lower = jnp.linalg.cholesky(gram, symmetrize_input=False)]
    dot_general x11 -> x2, matrix products: 35.5 us -> 23.8 us  [inner_dot(): return lax.dot_general(left, right, (((0,), (0,)), ((), ())), precision=HI)]
  transfers between devices with their start and end apart: 12 -> 3, of which waited for: 12 -> 3; matrix products, arithmetic and copies ran while one was open for 0% -> 0% of each run, Pallas kernels for 0% -> 0%
where the time goes in v1:
time: 647 us; the launch traced here: 636 us
  other arithmetic  261 us (40%)
  waiting for transfers between devices  210 us (32%)
  matrix products  59.2 us (9%)
  blocking collectives  52.7 us (8%)
  local copies, waits for them, and re-layouts  34.8 us (5%)
  between operations  18.8 us (3%)
    another operation x30, other arithmetic, on_device(): lower = jnp.linalg.cholesky(gram, symmetrize_input=False)  173 us
    all_gather x1, waiting for transfers between devices, on_device(): gram = lax.all_gather(gram_part, 'col', tiled=True)  84.7 us
    another operation x3, other arithmetic, on_device(): factor = jax.scipy.linalg.solve_triangular(lower, rhs, lower=True)  83.5 us
    all_gather x1, waiting for transfers between devices, on_device(): panels = lax.all_gather(mine, 'col')  78.4 us
    all_to_all x1, blocking collectives, on_device(): lax.all_to_all(pieces, 'col', split_axis=0, concat_axis=0, tiled=True)  52.7 us
    psum x1, waiting for transfers between devices, on_device(): rhs = lax.psum(inner_dot(panels, stacked), 'row')  46.4 us
    dot_general x2, matrix products, inner_dot(): return lax.dot_general(left, right, (((0,), (0,)), ((), ())), precision=HI)  23.8 us
    another operation x14, matrix products, on_device(): lower = jnp.linalg.cholesky(gram, symmetrize_input=False)  23.3 us
  transfers between devices with their start and end apart: 3, of which 3 were waited for; matrix products, arithmetic and copies ran while one was open for 0% of the time, Pallas kernels for 0%

profile of v1, /device:TPU:1, one launch (start us, length us, event | category | flops | bytes accessed | tf_op | source)
XLA Modules:
  0.0 636.5 jit_solution(12063077370027670616)
XLA Ops:
  7.3 1.4 broadcast_multiply_fusion
  8.7 2.1 pad_maximum_fusion
  10.8 1.4 reshape.90
  12.2 52.7 %all_to_all.5 = f32[64,20,256]{2,1,0:T(8,128)S(1)} all-to-all(f32[64,20,256]{2,1,0:T(8,128)S(1)} %reshape.90), channel_id=1, replica_groups=mesh['col'=64,'row'=4] {'col'}, dimensions={0} | all-to-all | bytes 2621440 | tf_op jit(solution)/shard_map/all_to_all | solution.py:34
  65.7 78.4 %all-gather.6.cloned.1.call-done = f32[256,20,256]{2,1,0:T(8,128)} async-done(((f32[4,20,256]{2,1,0:T(8,128)}), f32[256,20,256]{2,1,0:T(8,128)}) %all-gather.6.cloned.1.call-update) | async-done | bytes 5242896 | tf_op jit(solution)/shard_map/all_gather | solution.py:36
  144.1 5.2 copy.5
  149.2 1.3 copy.6
  150.5 9.5 %fusion.63 = f32[1024,256]{1,0:T(8,128)} fusion(f32[1280,1024]{1,0:T(8,128)S(1)} %bitcast.108, f32[1024,256]{1,0:T(8,128)S(1)} %broadcast_multiply_fusion, f32[256,256]{1,0:T(8,128)S(1)} %copy-done), kind=kOutput, calls=%fused_computation.162 | convolution fusion | flops 4026859520 | bytes 7602176 | tf_op jit(solution)/shard_map/dot_general | solution.py:13
  160.1 14.3 %fusion.5 = f32[16,1024]{1,0:T(8,128)} fusion(f32[1280,1024]{1,0:T(8,128)S(1)} %bitcast.109, s32[]{:T(128)S(6)} %select_n.14), kind=kOutput, calls=%fused_computation.31 | convolution fusion | flops 251658240 | bytes 5963780 | tf_op jit(solution)/shard_map/dot_general | solution.py:13
  174.4 46.4 %all-reduce.4.cloned.1.call-done = (f32[1024,256]{1,0:T(8,128)}, f32[16,1024]{1,0:T(8,128)}) async-done(((f32[1024,256]{1,0:T(8,128)}, f32[16,1024]{1,0:T(8,128)}), (f32[1024,256]{1,0:T(8,128)}, f32[16,1024]{1,0:T(8,128)})) %all-reduce.4.cloned.1.call-update) | async-done | bytes 1114128 | tf_op jit(solution)/shard_map/psum | solution.py:42
  220.8 84.7 %all-gather.4.cloned.1.call-done = f32[1024,1024]{1,0:T(8,128)} async-done(((f32[16,1024]{1,0:T(8,128)}), f32[1024,1024]{1,0:T(8,128)}) %all-gather.4.cloned.1.call-update) | async-done | bytes 4194320 | tf_op jit(solution)/shard_map/all_gather | solution.py:41
  305.5 0.8 cholesky.580
  306.4 11.7 %cholesky.223 = f32[128,128]{1,0:T(8,128)S(1)} custom-call(f32[128,128]{1,0:T(8,128)S(1)} %cholesky.580), custom_call_target="Cholesky" | custom-call | tf_op jit(solution)/shard_map/jit(cholesky)/cholesky | solution.py:43
  318.1 9.8 %custom-call.63 = f32[1,128,128]{1,2,0:T(8,128)S(1)} custom-call(f32[1,128,128]{2,1,0:T(8,128)S(1)} %get-tuple-element.71), custom_call_target="InvertDiagBlocksLowerTriangular" | custom-call | tf_op jit(solution)/shard_map/jit(cholesky)/cholesky | solution.py:43
  328.0 2.5 cholesky.255
  330.5 2.4 constant_dynamic-update-slice_fusion.31
  332.8 1.5 convolution_subtract_fusion
  334.4 11.7 %cholesky.244 = f32[128,128]{1,0:T(8,128)S(1)} custom-call(f32[128,128]{1,0:T(8,128)S(1)} %cholesky.584), custom_call_target="Cholesky" | custom-call | tf_op jit(solution)/shard_map/jit(cholesky)/cholesky | solution.py:43
  346.8 10.2 %custom-call.64 = f32[1,128,128]{1,2,0:T(8,128)S(1)} custom-call(f32[1,128,128]{2,1,0:T(8,128)S(1)} %get-tuple-element.68), custom_call_target="InvertDiagBlocksLowerTriangular" | custom-call | tf_op jit(solution)/shard_map/jit(cholesky)/cholesky | solution.py:43
  356.9 1.2 convolution_dynamic-update-slice_fusion
  358.2 2.1 convolution_subtract_fusion.1
  360.3 11.7 %cholesky.468 = f32[128,128]{1,0:T(8,128)S(1)} custom-call(f32[128,128]{1,0:T(8,128)S(1)} %cholesky.589), custom_call_target="Cholesky" | custom-call | tf_op jit(solution)/shard_map/jit(cholesky)/cholesky | solution.py:43
  372.6 0.7 compare_reduce_fusion.5
  373.4 9.8 %custom-call.65 = f32[1,128,128]{1,2,0:T(8,128)S(1)} custom-call(f32[1,128,128]{2,1,0:T(8,128)S(1)} %get-tuple-element.65), custom_call_target="InvertDiagBlocksLowerTriangular" | custom-call | tf_op jit(solution)/shard_map/jit(cholesky)/cholesky | solution.py:43
  383.2 1.2 convolution_dynamic-update-slice_fusion.1
  384.3 2.3 convolution_subtract_fusion.2
  386.7 11.9 %cholesky.487 = f32[128,128]{1,0:T(8,128)S(1)} custom-call(f32[128,128]{1,0:T(8,128)S(1)} %cholesky.594), custom_call_target="Cholesky" | custom-call | tf_op jit(solution)/shard_map/jit(cholesky)/cholesky | solution.py:43
  399.9 9.8 %custom-call.66 = f32[1,128,128]{1,2,0:T(8,128)S(1)} custom-call(f32[1,128,128]{2,1,0:T(8,128)S(1)} %get-tuple-element.62), custom_call_target="InvertDiagBlocksLowerTriangular" | custom-call | tf_op jit(solution)/shard_map/jit(cholesky)/cholesky | solution.py:43
  409.7 1.1 convolution_dynamic-update-slice_fusion.2
  410.8 2.3 convolution_subtract_fusion.3
  413.2 11.7 %cholesky.506 = f32[128,128]{1,0:T(8,128)S(1)} custom-call(f32[128,128]{1,0:T(8,128)S(1)} %cholesky.599), custom_call_target="Cholesky" | custom-call | tf_op jit(solution)/shard_map/jit(cholesky)/cholesky | solution.py:43
  425.5 0.7 compare_reduce_fusion.3
  426.2 9.8 %custom-call.67 = f32[1,128,128]{1,2,0:T(8,128)S(1)} custom-call(f32[1,128,128]{2,1,0:T(8,128)S(1)} %get-tuple-element.59), custom_call_target="InvertDiagBlocksLowerTriangular" | custom-call | tf_op jit(solution)/shard_map/jit(cholesky)/cholesky | solution.py:43
  436.0 1.0 convolution_dynamic-update-slice_fusion.3
  437.1 2.5 convolution_subtract_fusion.4
  439.6 11.7 %cholesky.526 = f32[128,128]{1,0:T(8,128)S(1)} custom-call(f32[128,128]{1,0:T(8,128)S(1)} %cholesky.604), custom_call_target="Cholesky" | custom-call | tf_op jit(solution)/shard_map/jit(cholesky)/cholesky | solution.py:43
  452.7 9.8 %custom-call.68 = f32[1,128,128]{1,2,0:T(8,128)S(1)} custom-call(f32[1,128,128]{2,1,0:T(8,128)S(1)} %get-tuple-element.56), custom_call_target="InvertDiagBlocksLowerTriangular" | custom-call | tf_op jit(solution)/shard_map/jit(cholesky)/cholesky | solution.py:43
  462.5 0.9 convolution_dynamic-update-slice_fusion.5
  463.4 2.0 convolution_subtract_fusion.11
  465.5 11.7 %cholesky.546 = f32[128,128]{1,0:T(8,128)S(1)} custom-call(f32[128,128]{1,0:T(8,128)S(1)} %cholesky.609), custom_call_target="Cholesky" | custom-call | tf_op jit(solution)/shard_map/jit(cholesky)/cholesky | solution.py:43
  478.5 10.2 %custom-call.69 = f32[1,128,128]{1,2,0:T(8,128)S(1)} custom-call(f32[1,128,128]{2,1,0:T(8,128)S(1)} %get-tuple-element.53), custom_call_target="InvertDiagBlocksLowerTriangular" | custom-call | tf_op jit(solution)/shard_map/jit(cholesky)/cholesky | solution.py:43
  488.6 0.8 convolution_dynamic-update-slice_fusion.6
  489.5 1.8 convolution_subtract_fusion.13
  491.3 11.7 %cholesky.564 = f32[128,128]{1,0:T(8,128)S(1)} custom-call(f32[128,128]{1,0:T(8,128)S(1)} %convolution_subtract_fusion.13), custom_call_target="Cholesky" | custom-call | tf_op jit(solution)/shard_map/jit(cholesky)/cholesky | solution.py:43
  503.6 0.7 compare_reduce_fusion
  510.1 4.9 select_select_fusion
  515.0 23.1 %while.1 = (s32[]{:T(128)}, f32[1024,1024]{1,0:T(8,128)}, s32[8,2]{0,1:T(2,128)S(1)}, f32[8,128,128]{2,1,0:T(8,128)S(1)}, s32[]{:T(128)}) while((s32[]{:T(128)}, f32[1024,1024]{1,0:T(8,128)}, s32[8,2]{0,1:T(2,128)S(1)}, f32[8,128,128]{2,1,0:T(8,128)S(1)}, s32[]{:T(128)}) %tuple.58), condition=%wide.while_cond, body=%wide.while_body.sunk | while | flops 2 | bytes 131181 | solution.py:44
  515.7 2.3 bitcast_dynamic-update-slice_fusion.2
  518.6 2.3 bitcast_dynamic-update-slice_fusion.2
  521.5 2.3 bitcast_dynamic-update-slice_fusion.2
  524.4 2.3 bitcast_dynamic-update-slice_fusion.2
  527.3 2.3 bitcast_dynamic-update-slice_fusion.2
  530.2 2.3 bitcast_dynamic-update-slice_fusion.2
  533.0 2.3 bitcast_dynamic-update-slice_fusion.2
  535.9 2.2 bitcast_dynamic-update-slice_fusion.2
  538.1 78.6 %custom-call.70 = f32[8,128,128]{1,2,0:T(8,128)S(1)} custom-call(f32[8,128,128]{2,1,0:T(8,128)S(1)} %get-tuple-element.12), custom_call_target="InvertDiagBlocksLowerTriangular" | custom-call | tf_op jit(solution)/shard_map/jit(_solve_triangular)/triangular_solve | solution.py:44
  617.1 1.1 convolution_subtract_fusion.10
  618.5 1.2 convolution_subtract_fusion.8
  620.0 1.3 convolution_subtract_fusion.7
  621.7 1.4 convolution_subtract_fusion.6
  623.4 1.5 convolution_subtract_fusion.5
  625.2 1.5 convolution_subtract_fusion.9
  627.0 1.6 convolution_subtract_fusion.12
  629.0 0.8 dynamic-slice_select_fusion
  (59 shorter events, 16.1 us)
Async XLA Ops:
  6.5 137.5 %all-gather.6.cloned.1.call-start = ((), (), s32[]{:S(2)}) async-start(), calls=%async_computation.2 | async-start | bytes 6389760 | tf_op jit(solution)/shard_map/all_gather | solution.py:36
  65.6 155.2 %all-reduce.4.cloned.1.call-start = ((), (), s32[]{:S(2)}) async-start(), calls=%async_computation.3 | async-start | bytes 2228224 | tf_op jit(solution)/shard_map/psum | solution.py:42
  149.2 1.3 copy-start
  174.4 131.2 %all-gather.4.cloned.1.call-start = ((), (), s32[]{:S(2)}) async-start(), calls=%async_computation.1 | async-start | bytes 4259840 | tf_op jit(solution)/shard_map/all_gather | solution.py:41
  510.1 106.6 %copy-start.1 = (f32[1024,256]{1,0:T(8,128)S(1)}, f32[1024,256]{1,0:T(8,128)}, u32[]{:S(2)}) copy-start(f32[1024,256]{1,0:T(8,128)} %get-tuple-element.21) | copy-start | bytes 3145732
Sparse Core Ops, SparseCore 0:
  65.7 78.2 all-gather.5
  174.5 46.2 all-reduce.3
  223.9 81.5 all-gather.3

commit v2 on v1

--- a/solution.py
+++ b/solution.py
@@ -1,12 +1,16 @@
 import jax
 import jax.numpy as jnp
 from jax import lax
+from jax.experimental import pallas as pl
+from jax.experimental.pallas import tpu as pltpu
 from jax.sharding import PartitionSpec as P
 
 B = 256
 P_SIZE = 4
 ARC_ROWS = 128
 HI = lax.Precision.HIGHEST
+TILE = 128
+GROUP = 16
 
 
 def inner_dot(left, right):
@@ -15,6 +19,86 @@
 
 def plain_dot(left, right):
     return jnp.dot(left, right, precision=HI)
+
+
+def eliminate_tile(work_ref, inv_ref):
+    row_of = lax.broadcasted_iota(jnp.int32, (GROUP, 2 * TILE), 0)
+    lane_of = lax.broadcasted_iota(jnp.int32, (GROUP, TILE), 1)
+    narrow_row = row_of[:, :TILE]
+    for start in range(0, TILE, GROUP):
+        panel = work_ref[start:start + GROUP, :]
+        spread = [
+            jnp.broadcast_to(panel[:, start + i:start + i + 1], (GROUP, TILE)) for i in range(GROUP)
+        ]
+        left, right = panel[:, :TILE], panel[:, TILE:]
+        pivots = jnp.ones((GROUP, TILE), jnp.float32)
+        for i in range(GROUP):
+            pivot = spread[i][i:i + 1, :]
+            pivots = jnp.where(narrow_row == i, jnp.broadcast_to(pivot, pivots.shape), pivots)
+            if i + 1 == GROUP:
+                break
+            scale = jnp.where(narrow_row > i, spread[i], 0.0) * (1.0 / pivot)
+            for later in range(i + 1, GROUP):
+                spread[later] = spread[later] - scale * spread[later][i:i + 1, :]
+            left = left - scale * left[i:i + 1, :]
+            right = right - scale * right[i:i + 1, :]
+        root = 1.0 / jnp.sqrt(pivots)
+        left, right = left * root, right * root
+        inv_ref[start:start + GROUP, :] = right
+        if start + GROUP < TILE:
+            rest = jnp.where(lane_of >= start + GROUP, left, 0.0)
+            both = jnp.concatenate([left, right], axis=1)
+            work_ref[...] = work_ref[...] - lax.dot_general(
+                rest, both, (((0,), (0,)), ((), ())), precision=HI, preferred_element_type=jnp.float32
+            )
+
+def inverse_kernel(gram_ref, out_ref, work_ref, inv_ref):
+    size = gram_ref.shape[0]
+    tiles = size // TILE
+    out_ref[...] = gram_ref[...]
+    eye = jnp.where(
+        lax.broadcasted_iota(jnp.int32, (TILE, TILE), 0)
+        == lax.broadcasted_iota(jnp.int32, (TILE, TILE), 1), 1.0, 0.0
+    ).astype(jnp.float32)
+
+    def step(k, carry):
+        at = pl.multiple_of(k * TILE, TILE)
+        work_ref[:, :TILE] = out_ref[pl.ds(at, TILE), pl.ds(at, TILE)]
+        work_ref[:, TILE:] = eye
+        eliminate_tile(work_ref, inv_ref)
+        out_ref[pl.ds(at, TILE), pl.ds(at, TILE)] = eye
+        out_ref[pl.ds(at, TILE), :] = jnp.dot(
+            inv_ref[...], out_ref[pl.ds(at, TILE), :], precision=HI, preferred_element_type=jnp.float32
+        )
+
+        def update(i, inner):
+            below = pl.multiple_of(i * TILE, TILE)
+            out_ref[pl.ds(below, TILE), pl.ds(at, TILE)] = jnp.zeros((TILE, TILE), jnp.float32)
+            out_ref[pl.ds(below, TILE), :] = out_ref[pl.ds(below, TILE), :] - lax.dot_general(
+                out_ref[pl.ds(at, TILE), pl.ds(below, TILE)],
+                out_ref[pl.ds(at, TILE), :],
+                (((0,), (0,)), ((), ())),
+                precision=HI,
+                preferred_element_type=jnp.float32,
+            )
+            return inner
+
+        lax.fori_loop(k + 1, tiles, update, 0)
+        return carry
+
+    lax.fori_loop(0, tiles, step, 0)
+
+def block_inverse(gram):
+    size = gram.shape[0]
+    return pl.pallas_call(
+        inverse_kernel,
+        out_shape=jax.ShapeDtypeStruct(gram.shape, jnp.float32),
+        in_specs=[pl.BlockSpec(memory_space=pltpu.VMEM)],
+        out_specs=pl.BlockSpec(memory_space=pltpu.VMEM),
+        scratch_shapes=[pltpu.VMEM((TILE, 2 * TILE), jnp.float32), pltpu.VMEM((TILE, TILE), jnp.float32)],
+        cost_estimate=pl.CostEstimate(flops=8 * size**3, bytes_accessed=8 * size**2, transcendentals=0),
+        name="block_inverse",
+    )(gram)
 
 
 def on_device(r_slab, arc_rows, arc_blocks):
@@ -39,10 +123,14 @@
     own = lax.dynamic_slice(panels, (0, col_index * share), (height, share))
     gram_part = lax.psum(inner_dot(own, panels), "row")
     gram = lax.all_gather(gram_part, "col", tiled=True)
-    rhs = lax.psum(inner_dot(panels, stacked), "row")
-    lower = jnp.linalg.cholesky(gram, symmetrize_input=False)
-    factor = jax.scipy.linalg.solve_triangular(lower, rhs, lower=True)
-    mine_out = lax.dynamic_slice(factor, (row_index * B, 0), (B, B))
+    rhs, gram = lax.optimization_barrier((inner_dot(panels, stacked), gram))
+    rhs = lax.psum(rhs, "row")
+    inverse = block_inverse(gram)
+    inverse = lax.dynamic_slice(inverse, (row_index * B, 0), (B, lead))
+    tile_row = (row_index * B + lax.broadcasted_iota(jnp.int32, (B, lead), 0)) // TILE
+    tile_col = lax.broadcasted_iota(jnp.int32, (B, lead), 1) // TILE
+    inverse = jnp.where(tile_col <= tile_row, inverse, jnp.zeros_like(inverse))
+    mine_out = plain_dot(inverse, rhs)
     row_ids = row_index * B + lax.broadcasted_iota(jnp.int32, (B, B), 0)
     col_ids = col_index * B + lax.broadcasted_iota(jnp.int32, (B, B), 1)
     return jnp.where(col_ids >= row_ids, mine_out, jnp.zeros_like(mine_out))

time: 647 us -> 358 us (0.55); the launches traced: 636 us -> 357 us
  other arithmetic: 261 us -> 4.26 us
  Pallas kernels: 0 us -> 65.5 us
  matrix products: 59.2 us -> 18.7 us
  local copies, waits for them, and re-layouts: 34.8 us -> 10.8 us
  waiting for transfers between devices: 210 us -> 192 us
    another operation x33 -> x0, other arithmetic: 256 us -> none  [the longest x30 173 us: on_device(): lower = jnp.linalg.cholesky(gram, symmetrize_input=False)]
    pallas_call x0 -> x1, Pallas kernels: none -> 65.5 us  [block_inverse(): pl.pallas_call(inverse_kernel, out_shape=jax.ShapeDtypeStruct(gram.shape,...]
    another operation x29 -> x0, matrix products: 35.4 us -> none  [the longest x14 23.3 us: on_device(): lower = jnp.linalg.cholesky(gram, symmetrize_input=False)]
    another operation x33 -> x0, local copies, waits for them, and re-layouts: 26.2 us -> none
    all_gather x1, waiting for transfers between devices: 84.7 us -> 73.1 us  [on_device(): gram = lax.all_gather(gram_part, 'col', tiled=True)]
    dot_general x2, matrix products: 23.8 us -> 15.3 us  [inner_dot(): return lax.dot_general(left, right, (((0,), (0,)), ((), ())), precision=HI)]
    psum x1 -> x2, waiting for transfers between devices: 46.4 us -> 40.2 us  [the longest x1 40.2 us: on_device(): gram_part = lax.psum(inner_dot(own, panels), 'row')]
  transfers between devices with their start and end apart: 3 -> 4, of which waited for: 3 -> 3; matrix products, arithmetic and copies ran while one was open for 0% -> 3% of each run, Pallas kernels for 0% -> 18%
where the time goes in v2:
time: 358 us; the launch traced here: 357 us
  waiting for transfers between devices  192 us (54%)
  Pallas kernels  65.5 us (18%)
  blocking collectives  52.7 us (15%)
  matrix products  18.7 us (5%)
  between operations  13.2 us (4%)
  local copies, waits for them, and re-layouts  10.8 us (3%)
  other arithmetic  4.26 us (1%)
    all_gather x1, waiting for transfers between devices, on_device(): panels = lax.all_gather(mine, 'col')  78.4 us
    all_gather x1, waiting for transfers between devices, on_device(): gram = lax.all_gather(gram_part, 'col', tiled=True)  73.1 us
    pallas_call x1, Pallas kernels, block_inverse(): pl.pallas_call(inverse_kernel, out_shape=jax.ShapeDtypeStruct(gram.shape,...  65.5 us
    all_to_all x1, blocking collectives, on_device(): lax.all_to_all(pieces, 'col', split_axis=0, concat_axis=0, tiled=True)  52.7 us
    psum x1, waiting for transfers between devices, on_device(): gram_part = lax.psum(inner_dot(own, panels), 'row')  40.2 us
    dot_general x2, matrix products, inner_dot(): return lax.dot_general(left, right, (((0,), (0,)), ((), ())), precision=HI)  15.3 us
  transfers between devices with their start and end apart: 4, of which 3 were waited for; matrix products, arithmetic and copies ran while one was open for 3% of the time, Pallas kernels for 18%

profile of v2, /device:TPU:1, one launch (start us, length us, event | category | flops | bytes accessed | tf_op | source)
XLA Modules:
  0.0 357.3 jit_solution(2530319852360606925)
XLA Ops:
  6.5 0.0 all-gather.6.cloned.1.call-start
  6.5 0.7 convert_bitcast_fusion
  7.2 0.1 broadcast_bitcast_fusion
  7.3 1.4 broadcast_multiply_fusion
  8.7 2.1 pad_maximum_fusion
  10.8 1.4 reshape.15
  12.2 52.7 %all_to_all.5 = f32[64,20,256]{2,1,0:T(8,128)S(1)} all-to-all(f32[64,20,256]{2,1,0:T(8,128)S(1)} %reshape.15), channel_id=1, replica_groups=mesh['col'=64,'row'=4] {'col'}, dimensions={0} | all-to-all | bytes 2621440 | tf_op jit(solution)/shard_map/all_to_all | solution.py:118
  65.0 0.6 slice.4
  65.6 0.0 all-gather.6.cloned.1.call-update
  65.6 0.0 all-reduce.3.cloned.1.call-start
  65.7 78.4 %all-gather.6.cloned.1.call-done = f32[256,20,256]{2,1,0:T(8,128)} async-done(((f32[4,20,256]{2,1,0:T(8,128)}), f32[256,20,256]{2,1,0:T(8,128)}) %all-gather.6.cloned.1.call-update) | async-done | bytes 5242896 | tf_op jit(solution)/shard_map/all_gather | solution.py:120
  144.1 5.2 %copy.5 = f32[64,4,20,256]{3,1,2,0:T(4,128)S(1)} copy(f32[64,4,20,256]{3,2,1,0:T(8,128)} %bitcast.15) | data formatting | bytes 10485760 | tf_op jit(solution)/shard_map/all_gather | solution.py:120
  149.3 1.3 copy.6
  150.6 0.0 copy-start
  150.6 0.0 copy-start.1
  150.6 2.3 copy-done
  152.9 3.6 fusion.2
  156.4 0.0 all-reduce.3.cloned.1.call-update
  156.5 0.0 all-gather.4.cloned.1.call-start
  156.5 40.2 %all-reduce.3.cloned.1.call-done = f32[16,1024]{1,0:T(8,128)} async-done(((f32[16,1024]{1,0:T(8,128)}), f32[16,1024]{1,0:T(8,128)}) %all-reduce.3.cloned.1.call-update) | async-done | bytes 65552 | tf_op jit(solution)/shard_map/psum | solution.py:124
  196.7 0.0 all-gather.4.cloned.1.call-update
  196.7 0.2 all-reduce.5.cloned.1.call-start
  197.0 0.0 copy-done.1
  197.0 11.7 %fusion.18 = f32[1024,256]{1,0:T(8,128)} fusion(f32[1280,1024]{1,0:T(8,128)} %bitcast.13, f32[1024,256]{1,0:T(8,128)S(1)} %broadcast_multiply_fusion, f32[256,256]{1,0:T(8,128)S(1)} %copy-done.1), kind=kOutput, calls=%fused_computation.35 | convolution fusion | flops 4026859520 | bytes 7602176 | tf_op jit(solution)/shard_map/dot_general | solution.py:17
  208.7 73.1 %all-gather.4.cloned.1.call-done.gram_ref = f32[1024,1024]{1,0:T(8,128)} async-done(((f32[16,1024]{1,0:T(8,128)}), f32[1024,1024]{1,0:T(8,128)}) %all-gather.4.cloned.1.call-update) | async-done | bytes 4194320 | tf_op jit(solution)/shard_map/all_gather | solution.py:125
  281.8 0.0 all-reduce.5.cloned.1.call-update
  281.9 65.5 %block_inverse.1 = f32[1024,1024]{1,0:T(8,128)} custom-call(f32[1024,1024]{1,0:T(8,128)} %all-gather.4.cloned.1.call-done.gram_ref), custom_call_target="tpu_custom_call" | custom-call | flops 8589934592 | bytes 8388608 | tf_op jit(solution)/shard_map/block_inverse/pallas_call | solution.py:93
  347.4 0.0 all-reduce.5.cloned.1.call-done
  347.4 3.4 convolution_select_fusion
  (6 shorter events, 0.0 us)
Async XLA Ops:
  6.5 137.6 %all-gather.6.cloned.1.call-start = ((), (), s32[]{:S(2)}) async-start(), calls=%async_computation.4 | async-start | bytes 6389760 | tf_op jit(solution)/shard_map/all_gather | solution.py:120
  65.6 131.0 %all-reduce.3.cloned.1.call-start = ((), (), s32[]{:S(2)}) async-start(), calls=%async_computation.1 | async-start | bytes 131072 | tf_op jit(solution)/shard_map/psum | solution.py:124
  150.6 2.3 copy-start
  150.6 46.4 %copy-start.1 = (f32[256,256]{1,0:T(8,128)S(1)}, f32[256,256]{1,0:T(8,128)}, u32[]{:S(2)}) copy-start(f32[256,256]{1,0:T(8,128)} %param.3) | copy-start | bytes 786436
  156.5 125.3 %all-gather.4.cloned.1.call-start = ((), (), s32[]{:S(2)}) async-start(), calls=%async_computation.2 | async-start | bytes 4259840 | tf_op jit(solution)/shard_map/all_gather | solution.py:125
  196.7 150.7 %all-reduce.5.cloned.1.call-start = ((), (), s32[]{:S(2)}) async-start(), calls=%async_computation.3 | async-start | bytes 2097152 | tf_op jit(solution)/shard_map/psum | solution.py:127
Sparse Core Ops, SparseCore 0:
  65.8 78.3 all-gather.5
  156.6 40.0 all-reduce.2
  199.9 81.9 all-gather.3
  284.1 46.5 all-reduce.4

commit v3 on v2

--- a/solution.py
+++ b/solution.py
@@ -11,6 +11,9 @@
 HI = lax.Precision.HIGHEST
 TILE = 128
 GROUP = 16
+X_CHIPS, Y_CHIPS, Z_CHIPS = 4, 4, 8
+HALVES = 2
+MESH = pl.DeviceIdType.MESH
 
 
 def inner_dot(left, right):
@@ -101,8 +104,248 @@
     )(gram)
 
 
+def ring_places():
+    me = lax.axis_index("col")
+    return me % 2, me // 2 // Z_CHIPS, (me // 2) % Z_CHIPS
+
+
+def col_of(core, y, z):
+    return (y * Z_CHIPS + z) * 2 + core
+
+
+def relay_rings(piece, send_sems, recv_sems):
+    core, y, z = ring_places()
+    sent = []
+
+    def pass_on(slot, src_y, src_z, to):
+        copy = pltpu.make_async_remote_copy(
+            src_ref=piece(core, src_y, src_z),
+            dst_ref=piece(core, src_y, src_z),
+            send_sem=send_sems.at[slot],
+            recv_sem=recv_sems.at[slot],
+            device_id={"col": to},
+            device_id_type=MESH,
+        )
+        copy.start()
+        sent.append(copy)
+
+    def arrived(slot, src_core, src_y, src_z):
+        here = piece(src_core, src_y, src_z)
+        pltpu.make_async_copy(here, here, recv_sems.at[slot]).wait()
+
+    z_up, z_down = (z + 1) % Z_CHIPS, (z + Z_CHIPS - 1) % Z_CHIPS
+    y_up, y_down = (y + 1) % Y_CHIPS, (y + Y_CHIPS - 1) % Y_CHIPS
+    y_far = (y + 2) % Y_CHIPS
+    twin = col_of(1 - core, y, z)
+    slots_z, slots_up, slots_down, slots_far, slots_twin = 0, 8, 16, 24, 32
+    order = [0, 1, 7, 2, 6, 3, 5, 4]
+
+    def source(back):
+        return (z + Z_CHIPS - back) % Z_CHIPS
+
+    def spread_y(back):
+        pass_on(slots_up + back, y, source(back), col_of(core, y_up, z))
+        pass_on(slots_down + back, y, source(back), col_of(core, y_down, z))
+        pass_on(slots_twin + back, y, source(back), twin)
+
+    def spread_far(back):
+        arrived(slots_up + back, core, y_down, source(back))
+        if back % 2 == 0:
+            pass_on(slots_far + back, y_down, source(back), col_of(core, y_up, z))
+        pass_on(slots_twin + 8 + back, y_down, source(back), twin)
+        arrived(slots_down + back, core, y_up, source(back))
+        if back % 2 == 1:
+            pass_on(slots_far + back, y_up, source(back), col_of(core, y_down, z))
+        pass_on(slots_twin + 16 + back, y_up, source(back), twin)
+
+    def spread_twin(back):
+        arrived(slots_far + back, core, y_far, source(back))
+        pass_on(slots_twin + 24 + back, y_far, source(back), twin)
+
+    pass_on(slots_z + 1, y, z, col_of(core, y, z_up))
+    pass_on(slots_z + 7, y, z, col_of(core, y, z_down))
+    spread_y(0)
+    for at, back in enumerate(order):
+        if back:
+            arrived(slots_z + back, core, y, source(back))
+            if back < 4:
+                pass_on(slots_z + back + 1, y, source(back), col_of(core, y, z_up))
+            if back > 5:
+                pass_on(slots_z + back - 1, y, source(back), col_of(core, y, z_down))
+            spread_y(back)
+        if at >= 2:
+            spread_far(order[at - 2])
+        if at >= 4:
+            spread_twin(order[at - 4])
+    for back in order[6:]:
+        spread_far(back)
+    for back in order[4:]:
+        spread_twin(back)
+    for back in order:
+        for kind, src_y in enumerate((y, y_down, y_up, y_far)):
+            arrived(slots_twin + 8 * kind + back, 1 - core, src_y, source(back))
+    for copy in sent:
+        copy.wait_send()
+
+
+def lead_kernel(block_ref, out_ref, own_sem, scatter_send, scatter_recv, send_sems, recv_sems):
+    core, y, z = ring_places()
+    chip = y * Z_CHIPS + z
+    chips = Y_CHIPS * Z_CHIPS
+    height = block_ref.shape[0] // chips
+    barrier = pltpu.get_barrier_semaphore()
+
+    def greet(step, carry):
+        other = (chip + step) % chips
+        pl.semaphore_signal(barrier, inc=1, device_id={"col": other * 2 + core}, device_id_type=MESH)
+        return carry
+
+    lax.fori_loop(1, chips, greet, 0)
+    pl.semaphore_signal(barrier, inc=1, device_id={"col": chip * 2 + 1 - core}, device_id_type=MESH)
+    pl.semaphore_wait(barrier, chips)
+
+    def rows(of_chip):
+        return pl.ds(pl.multiple_of(of_chip * height, 8), height)
+
+    def scatter_copy(half, to_chip, step):
+        return pltpu.make_async_remote_copy(
+            src_ref=block_ref.at[rows(to_chip), :],
+            dst_ref=out_ref.at[core, half, rows(to_chip), :],
+            send_sem=scatter_send.at[step],
+            recv_sem=scatter_recv.at[half],
+            device_id={"col": to_chip * 2 + core},
+            device_id_type=MESH,
+        )
+
+    for half in range(HALVES):
+
+        @pl.when(chip == half)
+        def _():
+            def push(step, carry):
+                scatter_copy(half, (half + step) % chips, step).start()
+                return carry
+
+            lax.fori_loop(1, chips, push, 0)
+            own = pltpu.make_async_copy(
+                block_ref.at[rows(half), :], out_ref.at[core, half, rows(half), :], own_sem
+            )
+            own.start()
+            own.wait()
+
+    for half in range(HALVES):
+
+        @pl.when(chip != half)
+        def _():
+            here = out_ref.at[core, half, rows(chip), :]
+            pltpu.make_async_copy(here, here, scatter_recv.at[half]).wait()
+
+    relay_rings(
+        lambda of_core, of_y, of_z: out_ref.at[of_core, :, rows(of_y * Z_CHIPS + of_z), :],
+        send_sems,
+        recv_sems,
+    )
+    for half in range(HALVES):
+
+        @pl.when(chip == half)
+        def _():
+            def drain(step, carry):
+                scatter_copy(half, (half + step) % chips, step).wait_send()
+                return carry
+
+            lax.fori_loop(1, chips, drain, 0)
+
+
+def gram_kernel(part_ref, out_ref, slots_ref, own_sem, row_send, row_recv, send_sems, recv_sems):
+    core, y, z = ring_places()
+    row = lax.axis_index("row")
+    height = part_ref.shape[0]
+    barrier = pltpu.get_barrier_semaphore()
+    for near in (
+        col_of(core, y, (z + 1) % Z_CHIPS),
+        col_of(core, y, (z + Z_CHIPS - 1) % Z_CHIPS),
+        col_of(core, (y + 1) % Y_CHIPS, z),
+        col_of(core, (y + Y_CHIPS - 1) % Y_CHIPS, z),
+        col_of(1 - core, y, z),
+    ):
+        pl.semaphore_signal(barrier, inc=1, device_id={"col": near}, device_id_type=MESH)
+    for step in range(1, X_CHIPS):
+        pl.semaphore_signal(barrier, inc=1, device_id={"row": (row + step) % X_CHIPS}, device_id_type=MESH)
+    pl.semaphore_wait(barrier, 5 + X_CHIPS - 1)
+    copies = []
+    for step in range(1, X_CHIPS):
+        copy = pltpu.make_async_remote_copy(
+            src_ref=part_ref,
+            dst_ref=slots_ref.at[row],
+            send_sem=row_send.at[step],
+            recv_sem=row_recv.at[step],
+            device_id={"row": (row + step) % X_CHIPS},
+            device_id_type=MESH,
+        )
+        copy.start()
+        copies.append(copy)
+    own = pltpu.make_async_copy(part_ref, slots_ref.at[row], own_sem)
+    own.start()
+    own.wait()
+    for step in range(1, X_CHIPS):
+        here = slots_ref.at[(row + X_CHIPS - step) % X_CHIPS]
+        pltpu.make_async_copy(here, here, row_recv.at[step]).wait()
+    total = slots_ref[0]
+    for other in range(1, X_CHIPS):
+        total = total + slots_ref[other]
+
+    def piece(of_core, of_y, of_z):
+        first = pl.multiple_of((of_y * Z_CHIPS + of_z) * height, 8)
+        return out_ref.at[of_core, pl.ds(first, height), :]
+
+    piece(core, y, z)[...] = total
+    relay_rings(piece, send_sems, recv_sems)
+    for copy in copies:
+        copy.wait_send()
+
+
+def spread_lead(block):
+    height, width = block.shape
+    chips = Y_CHIPS * Z_CHIPS
+    return pl.pallas_call(
+        lead_kernel,
+        out_shape=jax.ShapeDtypeStruct((2, HALVES, height, width), jnp.float32),
+        in_specs=[pl.BlockSpec(memory_space=pltpu.VMEM)],
+        out_specs=pl.BlockSpec(memory_space=pltpu.VMEM),
+        scratch_shapes=[
+            pltpu.SemaphoreType.DMA,
+            pltpu.SemaphoreType.DMA((chips,)),
+            pltpu.SemaphoreType.DMA((HALVES,)),
+            pltpu.SemaphoreType.DMA((64,)),
+            pltpu.SemaphoreType.DMA((64,)),
+        ],
+        compiler_params=pltpu.CompilerParams(collective_id=0, has_side_effects=True),
+        name="spread_lead",
+    )(block)
+
+
+def sum_gram(part):
+    height, width = part.shape
+    chips = Y_CHIPS * Z_CHIPS
+    return pl.pallas_call(
+        gram_kernel,
+        out_shape=jax.ShapeDtypeStruct((2, chips * height, width), jnp.float32),
+        in_specs=[pl.BlockSpec(memory_space=pltpu.VMEM)],
+        out_specs=pl.BlockSpec(memory_space=pltpu.VMEM),
+        scratch_shapes=[
+            pltpu.VMEM((X_CHIPS, height, width), jnp.float32),
+            pltpu.SemaphoreType.DMA,
+            pltpu.SemaphoreType.DMA((X_CHIPS,)),
+            pltpu.SemaphoreType.DMA((X_CHIPS,)),
+            pltpu.SemaphoreType.DMA((64,)),
+            pltpu.SemaphoreType.DMA((64,)),
+        ],
+        compiler_params=pltpu.CompilerParams(collective_id=1, has_side_effects=True),
+        name="sum_gram",
+    )(part)
+
+
 def on_device(r_slab, arc_rows, arc_blocks):
-    n_col = lax.axis_size("col")
+    n_col = 2 * Y_CHIPS * Z_CHIPS
     col_index = lax.axis_index("col")
     row_index = lax.axis_index("row")
     n_arcs, blocks_here = arc_blocks.shape
@@ -112,18 +355,21 @@
         arc_rows.shape
     )
     stacked = jnp.concatenate([r_slab, masked], axis=0)
-    height = stacked.shape[0]
-    part = height // n_col
-    pieces = stacked.reshape(n_col, part, B)
-    pieces = lax.all_to_all(pieces, "col", split_axis=0, concat_axis=0, tiled=True)
-    mine = pieces[:P_SIZE]
-    panels = lax.all_gather(mine, "col")
-    panels = panels.transpose(0, 2, 1, 3).reshape(height, lead)
+    panels = spread_lead(stacked)
     share = lead // n_col
-    own = lax.dynamic_slice(panels, (0, col_index * share), (height, share))
-    gram_part = lax.psum(inner_dot(own, panels), "row")
-    gram = lax.all_gather(gram_part, "col", tiled=True)
-    rhs, gram = lax.optimization_barrier((inner_dot(panels, stacked), gram))
+    row_start = (col_index % 2) * (lead // 2) + (col_index // 2) * share
+    block = row_start // B
+    own = lax.dynamic_slice(
+        panels, (block % 2, block // 2, 0, row_start % B), (1, 1, stacked.shape[0], share)
+    )[0, 0]
+    gram_part = jnp.concatenate(
+        [inner_dot(own, panels[j % 2, j // 2]) for j in range(P_SIZE)], axis=1
+    )
+    gram = sum_gram(gram_part).reshape(lead, lead)
+    rhs_part = jnp.concatenate(
+        [inner_dot(panels[j % 2, j // 2], stacked) for j in range(P_SIZE)], axis=0
+    )
+    rhs, gram = lax.optimization_barrier((rhs_part, gram))
     rhs = lax.psum(rhs, "row")
     inverse = block_inverse(gram)
     inverse = lax.dynamic_slice(inverse, (row_index * B, 0), (B, lead))

time: 358 us -> 216 us (0.60)
  waiting for transfers between devices: 192 us -> 0.02 us
  Pallas kernels: 65.5 us -> 169 us
  blocking collectives: 52.7 us -> 0 us
  local copies, waits for them, and re-layouts: 10.8 us -> 0.08 us
  matrix products: 18.7 us -> 27.6 us
    all_gather x2 -> x0, waiting for transfers between devices: 152 us -> none  [the longest x1 78.4 us: on_device(): panels = lax.all_gather(mine, 'col')]
    pallas_call x0 -> x2, Pallas kernels: none -> 104 us  [the longest x1 67.5 us: spread_lead(): pl.pallas_call(lead_kernel, out_shape=jax.ShapeDtypeStruct((2, HALVES, he...]
    all_to_all x1 -> x0, blocking collectives: 52.7 us -> none  [on_device(): lax.all_to_all(pieces, 'col', split_axis=0, concat_axis=0, tiled=True)]
    psum x1 -> x0, waiting for transfers between devices: 40.2 us -> none  [on_device(): gram_part = lax.psum(inner_dot(own, panels), 'row')]
    dot_general x2 -> x8, matrix products: 15.3 us -> 24.3 us  [inner_dot(): return lax.dot_general(left, right, (((0,), (0,)), ((), ())), precision=HI)]
    all_gather x1 -> x0, local copies, waits for them, and re-layouts: 5.17 us -> none  [on_device(): panels = lax.all_gather(mine, 'col')]
  transfers between devices with their start and end apart: 4 -> 1, of which waited for: 3 -> 0; matrix products, arithmetic and copies ran while one was open for 3% -> 0% of each run, Pallas kernels for 18% -> 30%
where the time goes in v3:
time: 216 us
  Pallas kernels  169 us (78%)
  matrix products  27.6 us (13%)
  between operations  13.6 us (6%)
  other arithmetic  5.03 us (2%)
    pallas_call x1, Pallas kernels, spread_lead(): pl.pallas_call(lead_kernel, out_shape=jax.ShapeDtypeStruct((2, HALVES, he...  67.5 us
    pallas_call x1, Pallas kernels, block_inverse(): pl.pallas_call(inverse_kernel, out_shape=jax.ShapeDtypeStruct(gram.shape,...  65.3 us
    pallas_call x1, Pallas kernels, sum_gram(): pl.pallas_call(gram_kernel, out_shape=jax.ShapeDtypeStruct((2, chips * he...  36.6 us
    dot_general x8, matrix products, inner_dot(): return lax.dot_general(left, right, (((0,), (0,)), ((), ())), precision=HI)  24.3 us
  transfers between devices with their start and end apart: 1, of which 0 were waited for; matrix products, arithmetic and copies ran while one was open for 0% of the time, Pallas kernels for 30%

profile of v3, /device:TPU:1, one launch (start us, length us, event | category | flops | bytes accessed | tf_op | source)
XLA Modules:
  0.0 215.8 jit_solution(14420541590194171648)
XLA Ops:
  6.5 0.0 copy-start.1
  6.5 0.0 all-reduce.2.cloned.1.call-start
  6.5 0.7 convert_bitcast_fusion
  7.2 0.1 broadcast_bitcast_fusion
  7.3 1.4 broadcast_multiply_fusion
  8.7 0.0 copy-done.1
  8.8 1.2 pad_maximum_fusion.block_ref
  9.9 67.5 %spread_lead.1 = f32[2,2,1280,256]{3,2,1,0:T(8,128)} custom-call(f32[1280,256]{1,0:T(8,128)} %pad_maximum_fusion.block_ref), custom_call_target="tpu_custom_call" | custom-call | tf_op jit(solution)/shard_map/spread_lead/pallas_call | solution.py:309
  77.4 0.0 copy-start
  77.4 3.7 %fusion.2 = f32[256,256]{1,0:T(8,128)S(1)} fusion(f32[2,2,1280,256]{3,2,1,0:T(8,128)} %spread_lead.1, f32[1024,256]{1,0:T(8,128)S(1)} %broadcast_multiply_fusion, f32[256,256]{1,0:T(8,128)S(1)} %copy-done.1), kind=kOutput, calls=%fused_computation.3 | convolution fusion | flops 1006960640 | bytes 2883584 | tf_op jit(solution)/shard_map/dot_general | solution.py:20
  81.1 3.5 %fusion.6 = f32[256,256]{1,0:T(8,128)S(1)} fusion(f32[2,2,1280,256]{3,2,1,0:T(8,128)} %spread_lead.1, f32[1024,256]{1,0:T(8,128)S(1)} %broadcast_multiply_fusion, f32[256,256]{1,0:T(8,128)S(1)} %copy-done.1), kind=kOutput, calls=%fused_computation.7 | convolution fusion | flops 1006960640 | bytes 2883584 | tf_op jit(solution)/shard_map/dot_general | solution.py:20
  84.7 0.0 copy-done
  84.7 2.2 %fusion.10 = f32[256,256]{1,0:T(8,128)S(1)} fusion(f32[2,2,1280,256]{3,2,1,0:T(8,128)S(1)} %copy-done, f32[1024,256]{1,0:T(8,128)S(1)} %broadcast_multiply_fusion, f32[256,256]{1,0:T(8,128)S(1)} %copy-done.1), kind=kOutput, calls=%fused_computation.11 | convolution fusion | flops 1006960640 | bytes 2883584 | tf_op jit(solution)/shard_map/dot_general | solution.py:20
  87.0 2.2 %fusion.14 = f32[256,256]{1,0:T(8,128)S(1)} fusion(f32[2,2,1280,256]{3,2,1,0:T(8,128)S(1)} %copy-done, f32[1024,256]{1,0:T(8,128)S(1)} %broadcast_multiply_fusion, f32[256,256]{1,0:T(8,128)S(1)} %copy-done.1), kind=kOutput, calls=%fused_computation.15 | convolution fusion | flops 1006960640 | bytes 2883584 | tf_op jit(solution)/shard_map/dot_general | solution.py:20
  89.3 3.1 %fusion = f32[16,256]{1,0:T(8,128)S(1)} fusion(f32[2,2,1280,256]{3,2,1,0:T(8,128)} %spread_lead.1, s32[]{:T(128)S(6)} %select_n.59, s32[]{:T(128)S(6)} %select_n.61, s32[]{:T(128)S(6)} %select_n.63), kind=kOutput, calls=%fused_computation.1 | convolution fusion | flops 62914560 | bytes 1982476 | tf_op jit(solution)/shard_map/dot_general | solution.py:20
  92.4 3.1 %fusion.4 = f32[16,256]{1,0:T(8,128)S(1)} fusion(f32[2,2,1280,256]{3,2,1,0:T(8,128)} %spread_lead.1, s32[]{:T(128)S(6)} %select_n.59, s32[]{:T(128)S(6)} %select_n.61, s32[]{:T(128)S(6)} %select_n.63), kind=kOutput, calls=%fused_computation.5 | convolution fusion | flops 62914560 | bytes 1982476 | tf_op jit(solution)/shard_map/dot_general | solution.py:20
  95.5 3.3 %fusion.8 = f32[16,256]{1,0:T(8,128)S(1)} fusion(f32[2,2,1280,256]{3,2,1,0:T(8,128)} %spread_lead.1, s32[]{:T(128)S(6)} %select_n.59, s32[]{:T(128)S(6)} %select_n.61, s32[]{:T(128)S(6)} %select_n.63), kind=kOutput, calls=%fused_computation.9 | convolution fusion | flops 62914560 | bytes 1982476 | tf_op jit(solution)/shard_map/dot_general | solution.py:20
  98.7 3.1 %fusion.12 = f32[16,256]{1,0:T(8,128)S(1)} fusion(f32[2,2,1280,256]{3,2,1,0:T(8,128)} %spread_lead.1, s32[]{:T(128)S(6)} %select_n.59, s32[]{:T(128)S(6)} %select_n.61, s32[]{:T(128)S(6)} %select_n.63), kind=kOutput, calls=%fused_computation.13 | convolution fusion | flops 62914560 | bytes 1982476 | tf_op jit(solution)/shard_map/dot_general | solution.py:20
  101.8 0.6 pad_maximum_fusion.2.part_ref
  102.5 36.6 %sum_gram.1 = f32[2,512,1024]{2,1,0:T(8,128)} custom-call(f32[16,1024]{1,0:T(8,128)} %pad_maximum_fusion.2.part_ref), custom_call_target="tpu_custom_call" | custom-call | tf_op jit(solution)/shard_map/sum_gram/pallas_call | solution.py:329
  139.1 1.0 pad_maximum_fusion.1
  140.1 0.0 all-reduce.2.cloned.1.call-update
  140.2 65.3 %block_inverse.1 = f32[1024,1024]{1,0:T(8,128)} custom-call(f32[1024,1024]{1,0:T(8,128)} %bitcast.35), custom_call_target="tpu_custom_call" | custom-call | flops 8589934592 | bytes 8388608 | tf_op jit(solution)/shard_map/block_inverse/pallas_call | solution.py:96
  205.6 0.0 all-reduce.2.cloned.1.call-done
  205.6 3.4 %convolution_select_fusion = f32[256,256]{1,0:T(8,128)} fusion(f32[1024,256]{1,0:T(8,128)} %all-reduce.2.cloned.1.call-done, f32[1024,1024]{1,0:T(8,128)} %block_inverse.1, s32[]{:T(128)S(6)} %select_n.64, s32[256]{0:T(256)S(1)} %get-tuple-element.9, s32[256]{0:T(256)S(1)} %get-tuple-element.14, s32[1024]{0:T(1024)S(1)} %get-tuple-element.11, ...), kind=kOutput, calls=%fused_computation.25 | convolution fusion | flops 806486016 | bytes 2372868 | tf_op jit(solution)/shard_map/dot_general | solution.py:24
  (5 shorter events, 0.0 us)
Async XLA Ops:
  6.5 2.2 %copy-start.1 = (f32[256,256]{1,0:T(8,128)S(1)}, f32[256,256]{1,0:T(8,128)}, u32[]{:S(2)}) copy-start(f32[256,256]{1,0:T(8,128)} %param.3) | copy-start | bytes 786436
  6.5 199.0 %all-reduce.2.cloned.1.call-start = ((), (), s32[]{:S(2)}) async-start(), calls=%async_computation | async-start | bytes 2097152 | tf_op jit(solution)/shard_map/psum | solution.py:373
  77.4 7.3 %copy-start = (f32[2,2,1280,256]{3,2,1,0:T(8,128)S(1)}, f32[2,2,1280,256]{3,2,1,0:T(8,128)}, u32[]{:S(2)}) copy-start(f32[2,2,1280,256]{3,2,1,0:T(8,128)} %spread_lead.1) | copy-start | bytes 15728644
Sparse Core Ops, SparseCore 0:
  140.3 44.1 all-reduce.1

commit v4 on v3

--- a/solution.py
+++ b/solution.py
@@ -55,10 +55,8 @@
                 rest, both, (((0,), (0,)), ((), ())), precision=HI, preferred_element_type=jnp.float32
             )
 
-def inverse_kernel(gram_ref, out_ref, work_ref, inv_ref):
-    size = gram_ref.shape[0]
-    tiles = size // TILE
-    out_ref[...] = gram_ref[...]
+def invert_blocks(mat_ref, work_ref, inv_ref, first, last):
+    tiles = mat_ref.shape[0] // TILE
     eye = jnp.where(
         lax.broadcasted_iota(jnp.int32, (TILE, TILE), 0)
         == lax.broadcasted_iota(jnp.int32, (TILE, TILE), 1), 1.0, 0.0
@@ -66,20 +64,20 @@
 
     def step(k, carry):
         at = pl.multiple_of(k * TILE, TILE)
-        work_ref[:, :TILE] = out_ref[pl.ds(at, TILE), pl.ds(at, TILE)]
+        work_ref[:, :TILE] = mat_ref[pl.ds(at, TILE), pl.ds(at, TILE)]
         work_ref[:, TILE:] = eye
         eliminate_tile(work_ref, inv_ref)
-        out_ref[pl.ds(at, TILE), pl.ds(at, TILE)] = eye
-        out_ref[pl.ds(at, TILE), :] = jnp.dot(
-            inv_ref[...], out_ref[pl.ds(at, TILE), :], precision=HI, preferred_element_type=jnp.float32
+        mat_ref[pl.ds(at, TILE), pl.ds(at, TILE)] = eye
+        mat_ref[pl.ds(at, TILE), :] = jnp.dot(
+            inv_ref[...], mat_ref[pl.ds(at, TILE), :], precision=HI, preferred_element_type=jnp.float32
         )
 
         def update(i, inner):
             below = pl.multiple_of(i * TILE, TILE)
-            out_ref[pl.ds(below, TILE), pl.ds(at, TILE)] = jnp.zeros((TILE, TILE), jnp.float32)
-            out_ref[pl.ds(below, TILE), :] = out_ref[pl.ds(below, TILE), :] - lax.dot_general(
-                out_ref[pl.ds(at, TILE), pl.ds(below, TILE)],
-                out_ref[pl.ds(at, TILE), :],
+            mat_ref[pl.ds(below, TILE), pl.ds(at, TILE)] = jnp.zeros((TILE, TILE), jnp.float32)
+            mat_ref[pl.ds(below, TILE), :] = mat_ref[pl.ds(below, TILE), :] - lax.dot_general(
+                mat_ref[pl.ds(at, TILE), pl.ds(below, TILE)],
+                mat_ref[pl.ds(at, TILE), :],
                 (((0,), (0,)), ((), ())),
                 precision=HI,
                 preferred_element_type=jnp.float32,
@@ -89,19 +87,95 @@
         lax.fori_loop(k + 1, tiles, update, 0)
         return carry
 
-    lax.fori_loop(0, tiles, step, 0)
-
-def block_inverse(gram):
+    lax.fori_loop(first, last, step, 0)
+
+
+def solve_kernel(
+    gram_ref, rhs_ref, out_ref, mat_ref, work_ref, inv_ref, slots_ref, sum_ref, own_sem,
+    part_send, part_recv, sum_send, sum_recv,
+):
+    row = lax.axis_index("row")
+    size = gram_ref.shape[0]
+    height = size // X_CHIPS
+    barrier = pltpu.get_barrier_semaphore()
+    for step in range(1, X_CHIPS):
+        pl.semaphore_signal(barrier, inc=1, device_id={"row": (row + step) % X_CHIPS}, device_id_type=MESH)
+    mat_ref[...] = gram_ref[...]
+    pl.semaphore_wait(barrier, X_CHIPS - 1)
+
+    def rows(of_row):
+        return pl.ds(pl.multiple_of(of_row * height, 8), height)
+
+    copies = []
+    for step in range(1, X_CHIPS):
+        peer = (row + step) % X_CHIPS
+        copy = pltpu.make_async_remote_copy(
+            src_ref=rhs_ref.at[rows(peer), :],
+            dst_ref=slots_ref.at[row],
+            send_sem=part_send.at[step],
+            recv_sem=part_recv.at[step],
+            device_id={"row": peer},
+            device_id_type=MESH,
+        )
+        copy.start()
+        copies.append(copy)
+    own = pltpu.make_async_copy(rhs_ref.at[rows(row), :], slots_ref.at[row], own_sem)
+    own.start()
+    own.wait()
+    invert_blocks(mat_ref, work_ref, inv_ref, 0, size // TILE // 2)
+    for step in range(1, X_CHIPS):
+        here = slots_ref.at[(row + X_CHIPS - step) % X_CHIPS]
+        pltpu.make_async_copy(here, here, part_recv.at[step]).wait()
+    total = slots_ref[0]
+    for other in range(1, X_CHIPS):
+        total = total + slots_ref[other]
+    sum_ref[rows(row), :] = total
+    for step in range(1, X_CHIPS):
+        copy = pltpu.make_async_remote_copy(
+            src_ref=sum_ref.at[rows(row), :],
+            dst_ref=sum_ref.at[rows(row), :],
+            send_sem=sum_send.at[step],
+            recv_sem=sum_recv.at[step],
+            device_id={"row": (row + step) % X_CHIPS},
+            device_id_type=MESH,
+        )
+        copy.start()
+        copies.append(copy)
+    invert_blocks(mat_ref, work_ref, inv_ref, size // TILE // 2, size // TILE)
+    for step in range(1, X_CHIPS):
+        here = sum_ref.at[rows((row + X_CHIPS - step) % X_CHIPS), :]
+        pltpu.make_async_copy(here, here, sum_recv.at[step]).wait()
+    tile_row = (row * height + lax.broadcasted_iota(jnp.int32, (height, size), 0)) // TILE
+    tile_col = lax.broadcasted_iota(jnp.int32, (height, size), 1) // TILE
+    inverse = jnp.where(tile_col <= tile_row, mat_ref[rows(row), :], 0.0)
+    out_ref[...] = jnp.dot(inverse, sum_ref[...], precision=HI, preferred_element_type=jnp.float32)
+    for copy in copies:
+        copy.wait_send()
+
+
+def solve_rows(gram, rhs):
     size = gram.shape[0]
+    height = size // X_CHIPS
     return pl.pallas_call(
-        inverse_kernel,
-        out_shape=jax.ShapeDtypeStruct(gram.shape, jnp.float32),
-        in_specs=[pl.BlockSpec(memory_space=pltpu.VMEM)],
+        solve_kernel,
+        out_shape=jax.ShapeDtypeStruct((height, rhs.shape[1]), jnp.float32),
+        in_specs=[pl.BlockSpec(memory_space=pltpu.VMEM)] * 2,
         out_specs=pl.BlockSpec(memory_space=pltpu.VMEM),
-        scratch_shapes=[pltpu.VMEM((TILE, 2 * TILE), jnp.float32), pltpu.VMEM((TILE, TILE), jnp.float32)],
-        cost_estimate=pl.CostEstimate(flops=8 * size**3, bytes_accessed=8 * size**2, transcendentals=0),
-        name="block_inverse",
-    )(gram)
+        scratch_shapes=[
+            pltpu.VMEM((size, size), jnp.float32),
+            pltpu.VMEM((TILE, 2 * TILE), jnp.float32),
+            pltpu.VMEM((TILE, TILE), jnp.float32),
+            pltpu.VMEM((X_CHIPS, height, rhs.shape[1]), jnp.float32),
+            pltpu.VMEM(rhs.shape, jnp.float32),
+            pltpu.SemaphoreType.DMA,
+            pltpu.SemaphoreType.DMA((X_CHIPS,)),
+            pltpu.SemaphoreType.DMA((X_CHIPS,)),
+            pltpu.SemaphoreType.DMA((X_CHIPS,)),
+            pltpu.SemaphoreType.DMA((X_CHIPS,)),
+        ],
+        compiler_params=pltpu.CompilerParams(collective_id=2, has_side_effects=True),
+        name="solve_rows",
+    )(gram, rhs)
 
 
 def ring_places():
@@ -113,7 +187,7 @@
     return (y * Z_CHIPS + z) * 2 + core
 
 
-def relay_rings(piece, send_sems, recv_sems):
+def relay_rings(piece, send_sems, recv_sems, fill=()):
     core, y, z = ring_places()
     sent = []
 
@@ -165,6 +239,8 @@
     pass_on(slots_z + 1, y, z, col_of(core, y, z_up))
     pass_on(slots_z + 7, y, z, col_of(core, y, z_down))
     spread_y(0)
+    for work in fill[:1]:
+        work()
     for at, back in enumerate(order):
         if back:
             arrived(slots_z + back, core, y, source(back))
@@ -181,6 +257,8 @@
         spread_far(back)
     for back in order[4:]:
         spread_twin(back)
+    for work in fill[1:]:
+        work()
     for back in order:
         for kind, src_y in enumerate((y, y_down, y_up, y_far)):
             arrived(slots_twin + 8 * kind + back, 1 - core, src_y, source(back))
@@ -255,10 +333,13 @@
             lax.fori_loop(1, chips, drain, 0)
 
 
-def gram_kernel(part_ref, out_ref, slots_ref, own_sem, row_send, row_recv, send_sems, recv_sems):
+def gram_kernel(
+    own_ref, panels_ref, block_ref, out_ref, rhs_ref, part_ref, slots_ref,
+    own_sem, row_send, row_recv, send_sems, recv_sems,
+):
     core, y, z = ring_places()
     row = lax.axis_index("row")
-    height = part_ref.shape[0]
+    height = own_ref.shape[1]
     barrier = pltpu.get_barrier_semaphore()
     for near in (
         col_of(core, y, (z + 1) % Z_CHIPS),
@@ -270,6 +351,21 @@
         pl.semaphore_signal(barrier, inc=1, device_id={"col": near}, device_id_type=MESH)
     for step in range(1, X_CHIPS):
         pl.semaphore_signal(barrier, inc=1, device_id={"row": (row + step) % X_CHIPS}, device_id_type=MESH)
+
+    def panel_dot(left_ref, j):
+        return lax.dot_general(
+            left_ref[...], panels_ref[j % 2, j // 2], (((0,), (0,)), ((), ())),
+            precision=HI, preferred_element_type=jnp.float32,
+        )
+
+    def rhs_dot(j):
+        rhs_ref[j * B:(j + 1) * B, :] = lax.dot_general(
+            panels_ref[j % 2, j // 2], block_ref[...], (((0,), (0,)), ((), ())),
+            precision=HI, preferred_element_type=jnp.float32,
+        )
+
+    for j in range(P_SIZE):
+        part_ref[:, j * B:(j + 1) * B] = panel_dot(own_ref, j)
     pl.semaphore_wait(barrier, 5 + X_CHIPS - 1)
     copies = []
     for step in range(1, X_CHIPS):
@@ -286,6 +382,8 @@
     own = pltpu.make_async_copy(part_ref, slots_ref.at[row], own_sem)
     own.start()
     own.wait()
+    rhs_dot(0)
+    rhs_dot(1)
     for step in range(1, X_CHIPS):
         here = slots_ref.at[(row + X_CHIPS - step) % X_CHIPS]
         pltpu.make_async_copy(here, here, row_recv.at[step]).wait()
@@ -298,7 +396,7 @@
         return out_ref.at[of_core, pl.ds(first, height), :]
 
     piece(core, y, z)[...] = total
-    relay_rings(piece, send_sems, recv_sems)
+    relay_rings(piece, send_sems, recv_sems, (lambda: rhs_dot(2), lambda: rhs_dot(3)))
     for copy in copies:
         copy.wait_send()
 
@@ -323,16 +421,21 @@
     )(block)
 
 
-def sum_gram(part):
-    height, width = part.shape
+def sum_gram(own, panels, block):
+    width = own.shape[1]
+    lead = P_SIZE * B
     chips = Y_CHIPS * Z_CHIPS
     return pl.pallas_call(
         gram_kernel,
-        out_shape=jax.ShapeDtypeStruct((2, chips * height, width), jnp.float32),
-        in_specs=[pl.BlockSpec(memory_space=pltpu.VMEM)],
-        out_specs=pl.BlockSpec(memory_space=pltpu.VMEM),
+        out_shape=(
+            jax.ShapeDtypeStruct((2, chips * width, lead), jnp.float32),
+            jax.ShapeDtypeStruct((lead, B), jnp.float32),
+        ),
+        in_specs=[pl.BlockSpec(memory_space=pltpu.VMEM)] * 3,
+        out_specs=[pl.BlockSpec(memory_space=pltpu.VMEM)] * 2,
         scratch_shapes=[
-            pltpu.VMEM((X_CHIPS, height, width), jnp.float32),
+            pltpu.VMEM((width, lead), jnp.float32),
+            pltpu.VMEM((X_CHIPS, width, lead), jnp.float32),
             pltpu.SemaphoreType.DMA,
             pltpu.SemaphoreType.DMA((X_CHIPS,)),
             pltpu.SemaphoreType.DMA((X_CHIPS,)),
@@ -341,7 +444,7 @@
         ],
         compiler_params=pltpu.CompilerParams(collective_id=1, has_side_effects=True),
         name="sum_gram",
-    )(part)
+    )(own, panels, block)
 
 
 def on_device(r_slab, arc_rows, arc_blocks):
@@ -362,21 +465,8 @@
     own = lax.dynamic_slice(
         panels, (block % 2, block // 2, 0, row_start % B), (1, 1, stacked.shape[0], share)
     )[0, 0]
-    gram_part = jnp.concatenate(
-        [inner_dot(own, panels[j % 2, j // 2]) for j in range(P_SIZE)], axis=1
-    )
-    gram = sum_gram(gram_part).reshape(lead, lead)
-    rhs_part = jnp.concatenate(
-        [inner_dot(panels[j % 2, j // 2], stacked) for j in range(P_SIZE)], axis=0
-    )
-    rhs, gram = lax.optimization_barrier((rhs_part, gram))
-    rhs = lax.psum(rhs, "row")
-    inverse = block_inverse(gram)
-    inverse = lax.dynamic_slice(inverse, (row_index * B, 0), (B, lead))
-    tile_row = (row_index * B + lax.broadcasted_iota(jnp.int32, (B, lead), 0)) // TILE
-    tile_col = lax.broadcasted_iota(jnp.int32, (B, lead), 1) // TILE
-    inverse = jnp.where(tile_col <= tile_row, inverse, jnp.zeros_like(inverse))
-    mine_out = plain_dot(inverse, rhs)
+    gram, rhs = sum_gram(own, panels, stacked)
+    mine_out = solve_rows(gram.reshape(lead, lead), rhs)
     row_ids = row_index * B + lax.broadcasted_iota(jnp.int32, (B, B), 0)
     col_ids = col_index * B + lax.broadcasted_iota(jnp.int32, (B, B), 1)
     return jnp.where(col_ids >= row_ids, mine_out, jnp.zeros_like(mine_out))

time: 216 us -> 183 us (0.85)
  matrix products: 27.6 us -> 0 us
  between operations: 13.6 us -> 0.06 us
  Pallas kernels: 169 us -> 175 us
  local copies, waits for them, and re-layouts: 0.08 us -> 2.48 us
    dot_general x9 -> x0, matrix products: 27.6 us -> none  [the longest x8 24.3 us: inner_dot(): return lax.dot_general(left, right, (((0,), (0,)), ((), ())), precision=HI)]
    pallas_call x2, Pallas kernels: 102 us -> 107 us  [the longest x1 66.9 us: solve_rows(): pl.pallas_call(solve_kernel, out_shape=jax.ShapeDtypeStruct((height, rhs....]
    squeeze x0 -> x1, local copies, waits for them, and re-layouts: none -> 2.4 us  [on_device(): lax.dynamic_slice(panels, (block % 2, block // 2, 0, row_start % B), (1,...]
  transfers between devices with their start and end apart: 1 -> 0, of which waited for: 0 -> 0; matrix products, arithmetic and copies ran while one was open for 0% -> 0% of each run, Pallas kernels for 30% -> 0%
where the time goes in v4:
time: 183 us; the launch traced here: 182 us
  Pallas kernels  175 us (96%)
  other arithmetic  5.03 us (3%)
  local copies, waits for them, and re-layouts  2.48 us (1%)
    pallas_call x1, Pallas kernels, spread_lead(): pl.pallas_call(lead_kernel, out_shape=jax.ShapeDtypeStruct((2, HALVES, he...  67.5 us
    pallas_call x1, Pallas kernels, solve_rows(): pl.pallas_call(solve_kernel, out_shape=jax.ShapeDtypeStruct((height, rhs....  66.9 us
    pallas_call x1, Pallas kernels, sum_gram(): pl.pallas_call(gram_kernel, out_shape=(jax.ShapeDtypeStruct((2, chips * w...  40.4 us

profile of v4, /device:TPU:1, one launch (start us, length us, event | category | flops | bytes accessed | tf_op | source)
XLA Modules:
  0.0 182.4 jit_solution(6523251727956885844)
XLA Ops:
  0.0 0.0 copy-start
  0.0 0.7 convert_bitcast_fusion
  0.7 0.1 broadcast_bitcast_fusion
  0.8 1.4 broadcast_multiply_fusion
  2.2 0.0 copy-done
  2.2 1.2 pad_maximum_fusion.block_ref
  3.4 67.5 %spread_lead.1.panels_ref = f32[2,2,1280,256]{3,2,1,0:T(8,128)} custom-call(f32[1280,256]{1,0:T(8,128)} %pad_maximum_fusion.block_ref), custom_call_target="tpu_custom_call" | custom-call | tf_op jit(solution)/shard_map/spread_lead/pallas_call | solution.py:407
  70.9 2.4 %dynamic-slice_bitcast_fusion.own_ref = f32[1280,16]{1,0:T(8,128)} fusion(f32[2,2,1280,256]{3,2,1,0:T(8,128)} %spread_lead.1.panels_ref, s32[]{:T(128)S(6)} %select_n.42, s32[]{:T(128)S(6)} %select_n.44, s32[]{:T(128)S(6)} %select_n.46), kind=kLoop, calls=%fused_computation.1 | loop fusion | bytes 163852 | tf_op jit(solution)/shard_map/squeeze | solution.py:465
  73.3 40.4 %sum_gram.1 = (f32[2,512,1024]{2,1,0:T(8,128)}, f32[1024,256]{1,0:T(8,128)}) custom-call(f32[1280,16]{1,0:T(8,128)} %dynamic-slice_bitcast_fusion.own_ref, f32[2,2,1280,256]{3,2,1,0:T(8,128)} %spread_lead.1.panels_ref, f32[1280,256]{1,0:T(8,128)} %pad_maximum_fusion.block_ref), custom_call_target="tpu_custom_call" | custom-call | tf_op jit(solution)/shard_map/sum_gram/pallas_call | solution.py:428
  113.7 66.9 %solve_rows.1 = f32[256,256]{1,0:T(8,128)} custom-call(f32[1024,1024]{1,0:T(8,128)} %bitcast.7, f32[1024,256]{1,0:T(8,128)} %get-tuple-element.8.rhs_ref), custom_call_target="tpu_custom_call" | custom-call | tf_op jit(solution)/shard_map/solve_rows/pallas_call | solution.py:159
  180.6 1.8 compare_select_fusion
  (1 shorter events, 0.0 us)
Async XLA Ops:
  0.0 2.2 %copy-start = (f32[256,256]{1,0:T(8,128)S(1)}, f32[256,256]{1,0:T(8,128)}, u32[]{:S(2)}) copy-start(f32[256,256]{1,0:T(8,128)} %param.3) | copy-start | bytes 786436

commit v5 on v4

--- a/solution.py
+++ b/solution.py
@@ -266,7 +266,10 @@
         copy.wait_send()
 
 
-def lead_kernel(block_ref, out_ref, own_sem, scatter_send, scatter_recv, send_sems, recv_sems):
+def lead_kernel(
+    block_ref, out_ref, pass_ref, far_ref, own_sem, out_send, direct_recv, pass_recv, far_recv,
+    pass_send, far_send, send_sems, recv_sems,
+):
     core, y, z = ring_places()
     chip = y * Z_CHIPS + z
     chips = Y_CHIPS * Z_CHIPS
@@ -285,52 +288,96 @@
     def rows(of_chip):
         return pl.ds(pl.multiple_of(of_chip * height, 8), height)
 
-    def scatter_copy(half, to_chip, step):
-        return pltpu.make_async_remote_copy(
-            src_ref=block_ref.at[rows(to_chip), :],
-            dst_ref=out_ref.at[core, half, rows(to_chip), :],
-            send_sem=scatter_send.at[step],
-            recv_sem=scatter_recv.at[half],
-            device_id={"col": to_chip * 2 + core},
-            device_id_type=MESH,
-        )
-
+    def send(source, target, send_sem, recv_sem, to_y, to_z):
+        copy = pltpu.make_async_remote_copy(
+            src_ref=source, dst_ref=target, send_sem=send_sem, recv_sem=recv_sem,
+            device_id={"col": col_of(core, to_y, to_z)}, device_id_type=MESH,
+        )
+        copy.start()
+        return copy
+
+    def arrived(here, sem):
+        pltpu.make_async_copy(here, here, sem).wait()
+
+    ahead = (4, 3, 5, 2, 6, 1, 7)
     for half in range(HALVES):
 
-        @pl.when(chip == half)
+        def place(of_y, step):
+            return of_y * Z_CHIPS + (half + step) % Z_CHIPS
+
+        def final(of_y, step):
+            return out_ref.at[core, half, rows(place(of_y, step)), :]
+
+        @pl.when((z == half) & (y == 0))
         def _():
-            def push(step, carry):
-                scatter_copy(half, (half + step) % chips, step).start()
-                return carry
-
-            lax.fori_loop(1, chips, push, 0)
-            own = pltpu.make_async_copy(
-                block_ref.at[rows(half), :], out_ref.at[core, half, rows(half), :], own_sem
-            )
+            copies = []
+
+            def push(source, target, recv_sem, to_y, to_z):
+                copies.append(send(source, target, out_send.at[len(copies)], recv_sem, to_y, to_z))
+
+            def held(of_y, step):
+                return block_ref.at[rows(place(of_y, step)), :]
+
+            for step in ahead:
+                via, slot = (1, step // 2) if step % 2 else (3, step // 2)
+                push(held(2, step), far_ref.at[slot], far_recv.at[slot], via, half)
+                for to_y in (1, 3):
+                    push(held(to_y, step), pass_ref.at[step], pass_recv.at[step], to_y, half)
+                to_z = (half + step) % Z_CHIPS
+                push(held(0, step), final(0, step), direct_recv.at[half], 0, to_z)
+            for to_y in (2, 1, 3):
+                push(held(to_y, 0), final(to_y, 0), direct_recv.at[half], to_y, half)
+            own = pltpu.make_async_copy(held(0, 0), final(0, 0), own_sem)
             own.start()
             own.wait()
+            for copy in copies:
+                copy.wait_send()
+
+        @pl.when((z == half) & (y != 0))
+        def _():
+            copies = []
+            for step in ahead:
+                for via in (1, 3):
+                    if step % 2 == (via == 1):
+
+                        @pl.when(y == via)
+                        def _():
+                            slot = step // 2
+                            arrived(far_ref.at[slot], far_recv.at[slot])
+                            send(
+                                far_ref.at[slot], pass_ref.at[step], far_send.at[slot],
+                                pass_recv.at[step], 2, half,
+                            )
+
+                arrived(pass_ref.at[step], pass_recv.at[step])
+                copies.append(
+                    send(
+                        pass_ref.at[step], final(y, step), pass_send.at[step],
+                        direct_recv.at[half], y, (half + step) % Z_CHIPS,
+                    )
+                )
+            for copy in copies:
+                copy.wait_send()
+            for step in ahead:
+                for via in (1, 3):
+                    if step % 2 == (via == 1):
+
+                        @pl.when(y == via)
+                        def _():
+                            slot = step // 2
+                            arrived(far_ref.at[slot], far_send.at[slot])
 
     for half in range(HALVES):
 
         @pl.when(chip != half)
         def _():
-            here = out_ref.at[core, half, rows(chip), :]
-            pltpu.make_async_copy(here, here, scatter_recv.at[half]).wait()
+            arrived(out_ref.at[core, half, rows(chip), :], direct_recv.at[half])
 
     relay_rings(
         lambda of_core, of_y, of_z: out_ref.at[of_core, :, rows(of_y * Z_CHIPS + of_z), :],
         send_sems,
         recv_sems,
     )
-    for half in range(HALVES):
-
-        @pl.when(chip == half)
-        def _():
-            def drain(step, carry):
-                scatter_copy(half, (half + step) % chips, step).wait_send()
-                return carry
-
-            lax.fori_loop(1, chips, drain, 0)
 
 
 def gram_kernel(
@@ -410,9 +457,15 @@
         in_specs=[pl.BlockSpec(memory_space=pltpu.VMEM)],
         out_specs=pl.BlockSpec(memory_space=pltpu.VMEM),
         scratch_shapes=[
+            pltpu.VMEM((Z_CHIPS, height // chips, width), jnp.float32),
+            pltpu.VMEM((4, height // chips, width), jnp.float32),
             pltpu.SemaphoreType.DMA,
             pltpu.SemaphoreType.DMA((chips,)),
             pltpu.SemaphoreType.DMA((HALVES,)),
+            pltpu.SemaphoreType.DMA((Z_CHIPS,)),
+            pltpu.SemaphoreType.DMA((4,)),
+            pltpu.SemaphoreType.DMA((Z_CHIPS,)),
+            pltpu.SemaphoreType.DMA((4,)),
             pltpu.SemaphoreType.DMA((64,)),
             pltpu.SemaphoreType.DMA((64,)),
         ],

time: 183 us -> 173 us (0.945)
  Pallas kernels: 175 us -> 165 us
    pallas_call x1, Pallas kernels: 67.5 us -> 60 us  [spread_lead(): pl.pallas_call(lead_kernel, out_shape=jax.ShapeDtypeStruct((2, HALVES, he...]
    pallas_call x1, Pallas kernels: 40.4 us -> 38.5 us  [sum_gram(): pl.pallas_call(gram_kernel, out_shape=(jax.ShapeDtypeStruct((2, chips * w...]
where the time goes in v5:
time: 173 us
  Pallas kernels  165 us (95%)
  other arithmetic  5.03 us (3%)
  local copies, waits for them, and re-layouts  2.48 us (1%)
    pallas_call x1, Pallas kernels, solve_rows(): pl.pallas_call(solve_kernel, out_shape=jax.ShapeDtypeStruct((height, rhs....  66.9 us
    pallas_call x1, Pallas kernels, spread_lead(): pl.pallas_call(lead_kernel, out_shape=jax.ShapeDtypeStruct((2, HALVES, he...  60 us
    pallas_call x1, Pallas kernels, sum_gram(): pl.pallas_call(gram_kernel, out_shape=(jax.ShapeDtypeStruct((2, chips * w...  38.5 us

profile of v5, /device:TPU:1, one launch (start us, length us, event | category | flops | bytes accessed | tf_op | source)
XLA Modules:
  0.0 172.9 jit_solution(15323328877638635272)
XLA Ops:
  0.0 0.0 copy-start
  0.0 0.7 convert_bitcast_fusion
  0.7 0.1 broadcast_bitcast_fusion
  0.8 1.4 broadcast_multiply_fusion
  2.2 0.0 copy-done
  2.2 1.2 pad_maximum_fusion.block_ref
  3.4 60.0 %spread_lead.1.panels_ref = f32[2,2,1280,256]{3,2,1,0:T(8,128)} custom-call(f32[1280,256]{1,0:T(8,128)} %pad_maximum_fusion.block_ref), custom_call_target="tpu_custom_call" | custom-call | tf_op jit(solution)/shard_map/spread_lead/pallas_call | solution.py:454
  63.3 2.4 %dynamic-slice_bitcast_fusion.own_ref = f32[1280,16]{1,0:T(8,128)} fusion(f32[2,2,1280,256]{3,2,1,0:T(8,128)} %spread_lead.1.panels_ref, s32[]{:T(128)S(6)} %select_n.42, s32[]{:T(128)S(6)} %select_n.44, s32[]{:T(128)S(6)} %select_n.46), kind=kLoop, calls=%fused_computation.1 | loop fusion | bytes 163852 | tf_op jit(solution)/shard_map/squeeze | solution.py:518
  65.7 38.5 %sum_gram.1 = (f32[2,512,1024]{2,1,0:T(8,128)}, f32[1024,256]{1,0:T(8,128)}) custom-call(f32[1280,16]{1,0:T(8,128)} %dynamic-slice_bitcast_fusion.own_ref, f32[2,2,1280,256]{3,2,1,0:T(8,128)} %spread_lead.1.panels_ref, f32[1280,256]{1,0:T(8,128)} %pad_maximum_fusion.block_ref), custom_call_target="tpu_custom_call" | custom-call | tf_op jit(solution)/shard_map/sum_gram/pallas_call | solution.py:481
  104.3 66.9 %solve_rows.1 = f32[256,256]{1,0:T(8,128)} custom-call(f32[1024,1024]{1,0:T(8,128)} %bitcast.7, f32[1024,256]{1,0:T(8,128)} %get-tuple-element.8.rhs_ref), custom_call_target="tpu_custom_call" | custom-call | tf_op jit(solution)/shard_map/solve_rows/pallas_call | solution.py:159
  171.2 1.8 %compare_select_fusion = f32[256,256]{1,0:T(8,128)} fusion(f32[256,256]{1,0:T(8,128)} %solve_rows.1, s32[256]{0:T(256)S(1)} %get-tuple-element.10, s32[256]{0:T(256)S(1)} %get-tuple-element.9), kind=kLoop, calls=%fused_computation.3 | loop fusion | flops 131072 | bytes 526336 | tf_op jit(solution)/shard_map/jit(_where)/select_n | solution.py:525
  (1 shorter events, 0.0 us)
Async XLA Ops:
  0.0 2.2 %copy-start = (f32[256,256]{1,0:T(8,128)S(1)}, f32[256,256]{1,0:T(8,128)}, u32[]{:S(2)}) copy-start(f32[256,256]{1,0:T(8,128)} %param.3) | copy-start | bytes 786436

commit v6 on v5

--- a/solution.py
+++ b/solution.py
@@ -10,7 +10,7 @@
 ARC_ROWS = 128
 HI = lax.Precision.HIGHEST
 TILE = 128
-GROUP = 16
+GROUP = 32
 X_CHIPS, Y_CHIPS, Z_CHIPS = 4, 4, 8
 HALVES = 2
 MESH = pl.DeviceIdType.MESH
@@ -310,10 +310,10 @@
 
         @pl.when((z == half) & (y == 0))
         def _():
-            copies = []
+            slots = iter(range(chips))
 
             def push(source, target, recv_sem, to_y, to_z):
-                copies.append(send(source, target, out_send.at[len(copies)], recv_sem, to_y, to_z))
+                send(source, target, out_send.at[next(slots)], recv_sem, to_y, to_z)
 
             def held(of_y, step):
                 return block_ref.at[rows(place(of_y, step)), :]
@@ -330,12 +330,9 @@
             own = pltpu.make_async_copy(held(0, 0), final(0, 0), own_sem)
             own.start()
             own.wait()
-            for copy in copies:
-                copy.wait_send()
 
         @pl.when((z == half) & (y != 0))
         def _():
-            copies = []
             for step in ahead:
                 for via in (1, 3):
                     if step % 2 == (via == 1):
@@ -350,22 +347,10 @@
                             )
 
                 arrived(pass_ref.at[step], pass_recv.at[step])
-                copies.append(
-                    send(
-                        pass_ref.at[step], final(y, step), pass_send.at[step],
-                        direct_recv.at[half], y, (half + step) % Z_CHIPS,
-                    )
+                send(
+                    pass_ref.at[step], final(y, step), pass_send.at[step],
+                    direct_recv.at[half], y, (half + step) % Z_CHIPS,
                 )
-            for copy in copies:
-                copy.wait_send()
-            for step in ahead:
-                for via in (1, 3):
-                    if step % 2 == (via == 1):
-
-                        @pl.when(y == via)
-                        def _():
-                            slot = step // 2
-                            arrived(far_ref.at[slot], far_send.at[slot])
 
     for half in range(HALVES):
 
@@ -378,6 +363,23 @@
         send_sems,
         recv_sems,
     )
+    for half in range(HALVES):
+
+        @pl.when((z == half) & (y == 0))
+        def _():
+            for slot in range(4 * len(ahead) + 3):
+                arrived(pass_ref.at[0], out_send.at[slot])
+
+        @pl.when((z == half) & (y != 0))
+        def _():
+            for step in ahead:
+                arrived(pass_ref.at[step], pass_send.at[step])
+                for via in (1, 3):
+                    if step % 2 == (via == 1):
+
+                        @pl.when(y == via)
+                        def _():
+                            arrived(far_ref.at[step // 2], far_send.at[step // 2])
 
 
 def gram_kernel(

time: 173 us -> 168 us (0.971)
  Pallas kernels: 165 us -> 160 us
    pallas_call x1, Pallas kernels: 66.9 us -> 61.6 us  [solve_rows(): pl.pallas_call(solve_kernel, out_shape=jax.ShapeDtypeStruct((height, rhs....]
where the time goes in v6:
time: 168 us
  Pallas kernels  160 us (95%)
  other arithmetic  5.03 us (3%)
  local copies, waits for them, and re-layouts  2.48 us (1%)
    pallas_call x1, Pallas kernels, solve_rows(): pl.pallas_call(solve_kernel, out_shape=jax.ShapeDtypeStruct((height, rhs....  61.6 us
    pallas_call x1, Pallas kernels, spread_lead(): pl.pallas_call(lead_kernel, out_shape=jax.ShapeDtypeStruct((2, HALVES, he...  60.1 us
    pallas_call x1, Pallas kernels, sum_gram(): pl.pallas_call(gram_kernel, out_shape=(jax.ShapeDtypeStruct((2, chips * w...  38.7 us

profile of v6, /device:TPU:1, one launch (start us, length us, event | category | flops | bytes accessed | tf_op | source)
XLA Modules:
  0.0 167.9 jit_solution(5421041570796604706)
XLA Ops:
  0.0 0.0 copy-start
  0.0 0.7 convert_bitcast_fusion
  0.7 0.1 broadcast_bitcast_fusion
  0.8 1.4 broadcast_multiply_fusion
  2.2 0.0 copy-done
  2.2 1.2 pad_maximum_fusion.block_ref
  3.4 60.1 %spread_lead.1.panels_ref = f32[2,2,1280,256]{3,2,1,0:T(8,128)} custom-call(f32[1280,256]{1,0:T(8,128)} %pad_maximum_fusion.block_ref), custom_call_target="tpu_custom_call" | custom-call | tf_op jit(solution)/shard_map/spread_lead/pallas_call | solution.py:456
  63.5 2.4 %dynamic-slice_bitcast_fusion.own_ref = f32[1280,16]{1,0:T(8,128)} fusion(f32[2,2,1280,256]{3,2,1,0:T(8,128)} %spread_lead.1.panels_ref, s32[]{:T(128)S(6)} %select_n.42, s32[]{:T(128)S(6)} %select_n.44, s32[]{:T(128)S(6)} %select_n.46), kind=kLoop, calls=%fused_computation.1 | loop fusion | bytes 163852 | tf_op jit(solution)/shard_map/squeeze | solution.py:520
  65.9 38.7 %sum_gram.1 = (f32[2,512,1024]{2,1,0:T(8,128)}, f32[1024,256]{1,0:T(8,128)}) custom-call(f32[1280,16]{1,0:T(8,128)} %dynamic-slice_bitcast_fusion.own_ref, f32[2,2,1280,256]{3,2,1,0:T(8,128)} %spread_lead.1.panels_ref, f32[1280,256]{1,0:T(8,128)} %pad_maximum_fusion.block_ref), custom_call_target="tpu_custom_call" | custom-call | tf_op jit(solution)/shard_map/sum_gram/pallas_call | solution.py:483
  104.5 61.6 %solve_rows.1 = f32[256,256]{1,0:T(8,128)} custom-call(f32[1024,1024]{1,0:T(8,128)} %bitcast.7, f32[1024,256]{1,0:T(8,128)} %get-tuple-element.8.rhs_ref), custom_call_target="tpu_custom_call" | custom-call | tf_op jit(solution)/shard_map/solve_rows/pallas_call | solution.py:159
  166.1 1.8 %compare_select_fusion = f32[256,256]{1,0:T(8,128)} fusion(f32[256,256]{1,0:T(8,128)} %solve_rows.1, s32[256]{0:T(256)S(1)} %get-tuple-element.10, s32[256]{0:T(256)S(1)} %get-tuple-element.9), kind=kLoop, calls=%fused_computation.3 | loop fusion | flops 131072 | bytes 526336 | tf_op jit(solution)/shard_map/jit(_where)/select_n | solution.py:527
  (1 shorter events, 0.0 us)
Async XLA Ops:
  0.0 2.2 %copy-start = (f32[256,256]{1,0:T(8,128)S(1)}, f32[256,256]{1,0:T(8,128)}, u32[]{:S(2)}) copy-start(f32[256,256]{1,0:T(8,128)} %param.3) | copy-start | bytes 786436

commit v7 on v6

--- a/solution.py
+++ b/solution.py
@@ -11,6 +11,7 @@
 HI = lax.Precision.HIGHEST
 TILE = 128
 GROUP = 32
+PAIR = 2 * TILE
 X_CHIPS, Y_CHIPS, Z_CHIPS = 4, 4, 8
 HALVES = 2
 MESH = pl.DeviceIdType.MESH
@@ -73,10 +74,14 @@
         )
 
         def update(i, inner):
-            below = pl.multiple_of(i * TILE, TILE)
-            mat_ref[pl.ds(below, TILE), pl.ds(at, TILE)] = jnp.zeros((TILE, TILE), jnp.float32)
-            mat_ref[pl.ds(below, TILE), :] = mat_ref[pl.ds(below, TILE), :] - lax.dot_general(
-                mat_ref[pl.ds(at, TILE), pl.ds(below, TILE)],
+            below = pl.multiple_of(i * PAIR, PAIR)
+            rows_here = below + lax.broadcasted_iota(jnp.int32, (PAIR, TILE), 0)
+            lanes_here = below + lax.broadcasted_iota(jnp.int32, (TILE, PAIR), 1)
+            old = mat_ref[pl.ds(below, PAIR), pl.ds(at, TILE)]
+            mat_ref[pl.ds(below, PAIR), pl.ds(at, TILE)] = jnp.where(rows_here >= at + TILE, 0.0, old)
+            factor = mat_ref[pl.ds(at, TILE), pl.ds(below, PAIR)]
+            mat_ref[pl.ds(below, PAIR), :] = mat_ref[pl.ds(below, PAIR), :] - lax.dot_general(
+                jnp.where(lanes_here >= at + TILE, factor, 0.0),
                 mat_ref[pl.ds(at, TILE), :],
                 (((0,), (0,)), ((), ())),
                 precision=HI,
@@ -84,7 +89,7 @@
             )
             return inner
 
-        lax.fori_loop(k + 1, tiles, update, 0)
+        lax.fori_loop((k + 1) // 2, tiles // 2, update, 0)
         return carry
 
     lax.fori_loop(first, last, step, 0)

time: 168 us -> 168 us (level)
  no operation moved by 1% of the time
where the time goes in v7:
time: 168 us; the launch traced here: 167 us
  Pallas kernels  160 us (95%)
  other arithmetic  5.03 us (3%)
  local copies, waits for them, and re-layouts  2.48 us (1%)
    pallas_call x1, Pallas kernels, solve_rows(): pl.pallas_call(solve_kernel, out_shape=jax.ShapeDtypeStruct((height, rhs....  61 us
    pallas_call x1, Pallas kernels, spread_lead(): pl.pallas_call(lead_kernel, out_shape=jax.ShapeDtypeStruct((2, HALVES, he...  60.1 us
    pallas_call x1, Pallas kernels, sum_gram(): pl.pallas_call(gram_kernel, out_shape=(jax.ShapeDtypeStruct((2, chips * w...  38.7 us

profile of v7, /device:TPU:1, one launch (start us, length us, event | category | flops | bytes accessed | tf_op | source)
XLA Modules:
  0.0 167.3 jit_solution(15272700158702285465)
XLA Ops:
  0.0 0.0 copy-start
  0.0 0.7 convert_bitcast_fusion
  0.7 0.1 broadcast_bitcast_fusion
  0.8 1.4 broadcast_multiply_fusion
  2.2 0.0 copy-done
  2.2 1.2 pad_maximum_fusion.block_ref
  3.4 60.1 %spread_lead.1.panels_ref = f32[2,2,1280,256]{3,2,1,0:T(8,128)} custom-call(f32[1280,256]{1,0:T(8,128)} %pad_maximum_fusion.block_ref), custom_call_target="tpu_custom_call" | custom-call | tf_op jit(solution)/shard_map/spread_lead/pallas_call | solution.py:461
  63.5 2.4 %dynamic-slice_bitcast_fusion.own_ref = f32[1280,16]{1,0:T(8,128)} fusion(f32[2,2,1280,256]{3,2,1,0:T(8,128)} %spread_lead.1.panels_ref, s32[]{:T(128)S(6)} %select_n.42, s32[]{:T(128)S(6)} %select_n.44, s32[]{:T(128)S(6)} %select_n.46), kind=kLoop, calls=%fused_computation.1 | loop fusion | bytes 163852 | tf_op jit(solution)/shard_map/squeeze | solution.py:525
  65.9 38.7 %sum_gram.1 = (f32[2,512,1024]{2,1,0:T(8,128)}, f32[1024,256]{1,0:T(8,128)}) custom-call(f32[1280,16]{1,0:T(8,128)} %dynamic-slice_bitcast_fusion.own_ref, f32[2,2,1280,256]{3,2,1,0:T(8,128)} %spread_lead.1.panels_ref, f32[1280,256]{1,0:T(8,128)} %pad_maximum_fusion.block_ref), custom_call_target="tpu_custom_call" | custom-call | tf_op jit(solution)/shard_map/sum_gram/pallas_call | solution.py:488
  104.5 61.0 %solve_rows.1 = f32[256,256]{1,0:T(8,128)} custom-call(f32[1024,1024]{1,0:T(8,128)} %bitcast.7, f32[1024,256]{1,0:T(8,128)} %get-tuple-element.8.rhs_ref), custom_call_target="tpu_custom_call" | custom-call | tf_op jit(solution)/shard_map/solve_rows/pallas_call | solution.py:164
  165.5 1.8 %compare_select_fusion = f32[256,256]{1,0:T(8,128)} fusion(f32[256,256]{1,0:T(8,128)} %solve_rows.1, s32[256]{0:T(256)S(1)} %get-tuple-element.10, s32[256]{0:T(256)S(1)} %get-tuple-element.9), kind=kLoop, calls=%fused_computation.3 | loop fusion | flops 131072 | bytes 526336 | tf_op jit(solution)/shard_map/jit(_where)/select_n | solution.py:532
  (1 shorter events, 0.0 us)
Async XLA Ops:
  0.0 2.2 %copy-start = (f32[256,256]{1,0:T(8,128)S(1)}, f32[256,256]{1,0:T(8,128)}, u32[]{:S(2)}) copy-start(f32[256,256]{1,0:T(8,128)} %param.3) | copy-start | bytes 786436
